TPU v7x, 128 devices: a whole 4x4x4 slice. The times are simulated.
128 devices in a mesh: gy: 32 (over y, x, core), gx: 4 (over z).
Axes of the slice: x: 4, y: 4, z: 4, core: 2. Of those that a mesh axis runs over, the one named last changes fastest.
Arguments:
- velocity: bfloat16 [3, 32, 1536, 1536], P(None, 'gy', 'gx'), may hold values from -40 to 40
- ref_planes: int32 [6], replicated, may hold values from 4 to 27, as said below
- partner_offsets: int32 [8], replicated, may hold values from -4 to 4, as said below
- band_owner: int32 [48], replicated, may hold values from 0 to 31, as said below
Outputs:
- correlations: float32 [96, 9, 384, 384], P('gy', None, 'gx')
Inputs may be any that keep to these rules, and one draw needn't show every extreme that they name: `ref_planes`: 6 distinct planes; 4 and 27 are among them. `partner_offsets`: 8 distinct offsets; -4 and 4 are among them. `band_owner`: the pairs owned by one index of gy are consecutive; no index owns more than 3 pairs and one owns exactly 3.
All inputs are finite; a program needn't handle non-finite values.
Results may differ from a plain program's by a relative error of at most 0.0035.
Values may be sent and summed in bfloat16 or wider, within the bound.
No kernel may reach another device: no remote copies, remote signals or barrier semaphores. Data moves between devices by JAX's collectives and lax.ppermute only.
A program may use at most 128 MiB of HBM per device.

v0:
```python
import math

import jax
import jax.numpy as jnp
from jax import lax
from jax.sharding import PartitionSpec as P


def angle_table(count_rows, count_cols, length, col_offset):
    rows = jnp.arange(count_rows, dtype=jnp.int32)
    cols = jnp.arange(count_cols, dtype=jnp.int32) + col_offset
    phase = rows[:, None] * cols[None, :] % length
    return 2.0 * math.pi / length * phase.astype(jnp.float32)


def x_transform(received, cos_x, sin_x):
    width_x = received.shape[-1]
    flat_rows = received.reshape(-1, width_x)
    cosine_part = jnp.dot(flat_rows, cos_x, preferred_element_type=jnp.float32).reshape(
        received.shape
    )
    sine_part = jnp.dot(flat_rows, sin_x, preferred_element_type=jnp.float32).reshape(
        received.shape
    )
    real_part = cosine_part[:, :, 0] + sine_part[:, :, 1]
    imag_part = cosine_part[:, :, 1] - sine_part[:, :, 0]
    return (real_part, imag_part)


def spread_left(left):
    return left.transpose(1, 0, 2, 3, 4, 5)[:, None, :, None]


def spread_right(right):
    return right.transpose(1, 2, 0, 3, 4, 5, 6)[:, :, None]


def per_device(velocity, ref_planes, partner_offsets, band_owner):
    highest = lax.Precision.HIGHEST
    row_count = lax.axis_size("gy")
    col_count = lax.axis_size("gx")
    devices = row_count * col_count
    comp_count, planes_dev, x_dev, width_z = velocity.shape
    width_x = x_dev * col_count
    half = width_z // 2
    lag_z = width_z // 4
    lag_x = width_x // 4
    block_len = lag_z // devices
    lag_block = lag_x // col_count
    row_id = lax.axis_index("gy")
    col_id = lax.axis_index("gx")
    norm_scale = 1.0 / float(width_x * width_z) ** 2
    z_angle = angle_table(width_z, half, width_z, 0)
    forward_z = jnp.concatenate([jnp.cos(z_angle), -jnp.sin(z_angle)], axis=1).astype(jnp.bfloat16)
    x_angle = angle_table(width_x, width_x, width_x, 0)
    cos_x = jnp.cos(x_angle).astype(jnp.bfloat16)
    sin_x = jnp.sin(x_angle).astype(jnp.bfloat16)
    along_z = jnp.einsum("cpxz,zq->cpqx", velocity, forward_z, preferred_element_type=jnp.float32)
    along_z = along_z.astype(jnp.bfloat16).reshape(comp_count, planes_dev, 2, 2, lag_z, x_dev)
    parcels = along_z.reshape(comp_count, planes_dev, 2, 2, devices, block_len, x_dev)
    parcels = parcels.transpose(4, 0, 1, 2, 3, 5, 6)
    item_rows = lax.all_to_all(parcels, ("gy", "gx"), split_axis=0, concat_axis=0, tiled=True)
    item_count = item_rows.shape[1]
    grouped = item_rows.reshape(
        row_count, col_count, item_count, planes_dev, 2, 2, block_len, x_dev
    )
    grouped = grouped.transpose(2, 0, 3, 4, 5, 6, 1, 7)
    grouped = grouped.reshape(item_count, row_count * planes_dev, 2, 2, block_len, width_x)
    real_part, imag_part = x_transform(grouped, cos_x, sin_x)
    block_start = (row_id * col_count + col_id) * block_len
    mode_index = (
        jnp.arange(2, dtype=jnp.int32)[:, None] * lag_z
        + block_start
        + jnp.arange(block_len, dtype=jnp.int32)[None, :]
    )
    weight = jnp.where(mode_index == 0, 1.0, 2.0).astype(jnp.float32)[None, None, :, :, None]
    ref_count = ref_planes.shape[0]
    off_count = partner_offsets.shape[0]
    pair_count = ref_count * off_count
    partner_index = (ref_planes[:, None] + partner_offsets[None, :]).reshape(-1)
    ref_real = (jnp.take(real_part, ref_planes, axis=1) * weight).reshape(
        comp_count, ref_count, 2, block_len, 4, lag_x
    )
    ref_imag = (jnp.take(imag_part, ref_planes, axis=1) * weight).reshape(
        comp_count, ref_count, 2, block_len, 4, lag_x
    )
    part_real = jnp.take(real_part, partner_index, axis=1).reshape(
        comp_count, ref_count, off_count, 2, block_len, 4, lag_x
    )
    part_imag = jnp.take(imag_part, partner_index, axis=1).reshape(
        comp_count, ref_count, off_count, 2, block_len, 4, lag_x
    )
    left_real = spread_left(ref_real)
    left_imag = spread_left(ref_imag)
    right_real = spread_right(part_real)
    right_imag = spread_right(part_imag)
    fold_real = jnp.sum(left_real * right_real + left_imag * right_imag, axis=(4, 6))
    fold_imag = jnp.sum(left_real * right_imag - left_imag * right_real, axis=(4, 6))
    fold_real = fold_real.reshape(pair_count, 9, block_len, lag_x)
    fold_imag = fold_imag.reshape(pair_count, 9, block_len, lag_x)
    slot_count = (2 * pair_count + row_count - 1) // row_count
    pair_order = jnp.arange(pair_count, dtype=jnp.int32)
    same_owner = band_owner[:, None] == band_owner[None, :]
    earlier = pair_order[None, :] < pair_order[:, None]
    slot_of = jnp.sum((same_owner & earlier).astype(jnp.int32), axis=1)
    dest_row = band_owner * slot_count + slot_of
    dest_table = (
        dest_row[None, :] == jnp.arange(row_count * slot_count, dtype=jnp.int32)[:, None]
    ).astype(jnp.float32)
    span_angle = angle_table(lag_z, lag_z, lag_z, 0)
    cos_span = jnp.cos(span_angle).reshape(devices, block_len, lag_z)
    sin_span = jnp.sin(span_angle).reshape(devices, block_len, lag_z)
    placed = jnp.dot(
        dest_table,
        jnp.stack([fold_real, fold_imag], axis=2).reshape(pair_count, -1),
        precision=highest,
    )
    placed = placed.reshape(row_count, slot_count, 9, 2, block_len, col_count, lag_block)
    placed = placed.transpose(0, 5, 1, 2, 3, 4, 6)
    buffer = placed.reshape(devices, slot_count, 9, 2, block_len * lag_block)
    arrived = lax.all_to_all(buffer, ("gy", "gx"), split_axis=0, concat_axis=0, tiled=True)
    arrived = arrived.reshape(devices, arrived.shape[1], 9, 2, block_len, lag_block)
    spec_real = arrived[:, :, :, 0]
    spec_imag = arrived[:, :, :, 1]
    spanwise_span_real = jnp.einsum(
        "dsqkl,dkz->sqlz", spec_real, cos_span, precision=highest
    ) - jnp.einsum("dsqkl,dkz->sqlz", spec_imag, sin_span, precision=highest)
    spanwise_span_imag = jnp.einsum(
        "dsqkl,dkz->sqlz", spec_real, sin_span, precision=highest
    ) + jnp.einsum("dsqkl,dkz->sqlz", spec_imag, cos_span, precision=highest)
    local_angle = angle_table(lag_x, lag_block, lag_x, col_id * lag_block)
    cos_local = jnp.cos(local_angle)
    sin_local = jnp.sin(local_angle)
    summed = jnp.einsum("ak,sqkz->asqz", cos_local, spanwise_span_real, precision=highest)
    summed = summed - jnp.einsum("ak,sqkz->asqz", sin_local, spanwise_span_imag, precision=highest)
    lagged = lax.psum_scatter(summed * norm_scale, "gx", scatter_dimension=0, tiled=True)
    return lagged.transpose(1, 2, 0, 3)


def solution(mesh):
    placed = (P(None, "gy", "gx", None), P(), P(), P())
    return jax.shard_map(
        per_device, mesh=mesh, in_specs=placed, out_specs=P("gy", None, "gx", None), check_vma=False
    )
```

profile of v0, /device:TPU:1, one launch (start us, length us, event | category | flops | bytes accessed | tf_op | source)
XLA Modules:
  0.0 725.6 jit_solution(14173614980125007050)
XLA Ops:
  6.5 0.0 copy-start
  6.5 19.6 %negate_convert_fusion = (bf16[1536,768]{0,1:T(8,128)(2,1)S(1)}, bf16[1536,768]{0,1:T(8,128)(2,1)S(1)}) fusion(), kind=kLoop, calls=%fused_computation.36 | loop fusion | flops 14155776 | bytes 4718592 | tf_op jit(solution)/shard_map/convert.1
  26.1 0.0 copy-done
  26.2 9.1 %fusion.42 = bf16[3,1,1536,384]{3,2,0,1:T(8,128)(2,1)} fusion(bf16[3,1,384,1536]{3,2,1,0:T(8,128)(2,1)S(1)} %copy-done, bf16[1536,768]{0,1:T(8,128)(2,1)S(1)} %get-tuple-element.15, bf16[1536,768]{0,1:T(8,128)(2,1)S(1)} %get-tuple-element.16), kind=kOutput, calls=%fused_computation.62 | convolution fusion | flops 5447024640 | bytes 11796480 | tf_op jit(solution)/shard_map/cpxz,zq->cpqx/dot_general | solution.py:58
  35.3 8.9 %reshape_reshape.4 = bf16[3,1,2,2,128,3,384]{6,5,4,3,2,0,1:T(4,128)(2,1)} reshape(bf16[3,1,1536,384]{3,2,0,1:T(8,128)(2,1)} %fusion.42) | data formatting | bytes 7077888 | tf_op jit(solution)/shard_map/reshape;reshape | solution.py:60
  44.2 9.6 %copy.60 = bf16[128,3,1,2,2,3,384]{6,4,5,3,2,1,0:T(2,128)(2,1)} copy(bf16[128,3,1,2,2,3,384]{6,5,0,4,3,1,2:T(4,128)(2,1)} %bitcast.164) | data formatting | bytes 7077888 | tf_op jit(solution)/shard_map/transpose | solution.py:61
  53.7 11.8 %all-to-all-start = ((bf16[128,3,1,2,2,3,384]{6,4,5,3,2,1,0:T(2,128)(2,1)}), bf16[128,3,1,2,2,3,384]{6,4,5,3,2,1,0:T(2,128)(2,1)S(1)}, u32[]{:S(2)}, u32[]{:S(2)}) async-start(bf16[128,3,1,2,2,3,384]{6,4,5,3,2,1,0:T(2,128)(2,1)} %copy.60), calls=%async_computation | async-start | bytes 7077888 | tf_op jit(solution)/shard_map/all_to_all | solution.py:62
  65.6 0.0 copy-done.8
  65.6 0.0 copy-done.7
  65.6 0.7 broadcast_add_fusion
  66.4 0.5 multiply_add_fusion.2
  66.9 0.1 add.177
  67.0 0.5 copy-done.9
  67.5 0.9 convert_reduce_fusion
  68.4 1.2 compare_and_fusion.1
  69.6 1.2 compare_and_fusion
  70.8 1.2 multiply_add_fusion.3
  72.0 0.6 fusion.100
  72.6 37.0 %fusion.140 = bf16[1536,1536,1,1,1,1]{1,0,5,4,3,2:T(8,128)(2,1)} fusion(), kind=kLoop, calls=%fused_computation.26.clone.clone.1 | loop fusion | flops 23592960 | bytes 4718592 | tf_op jit(solution)/shard_map/dot_general | solution.py:22
  109.6 36.7 %fusion.138 = bf16[1536,1536,1,1,1,1]{1,0,5,4,3,2:T(8,128)(2,1)} fusion(), kind=kLoop, calls=%fused_computation.24.clone.clone.1 | loop fusion | flops 23592960 | bytes 4718592 | tf_op jit(solution)/shard_map/dot_general | solution.py:19
  146.3 0.0 all-to-all-done
  146.3 3.6 copy.111
  149.9 5.6 dot_general.37
  155.4 7.5 %fusion.14 = f32[3,32,2,2,3,1536]{5,1,4,3,2,0:T(8,128)S(1)} fusion(bf16[3,32,2,2,3,1536]{5,1,4,3,2,0:T(8,128)(2,1)S(1)} %dot_general.37, bf16[1536,1536,1,1,1,1]{1,0,5,4,3,2:T(8,128)(2,1)} %fusion.140), kind=kOutput, calls=%fused_computation.27 | convolution fusion | flops 5435817984 | bytes 15335424 | tf_op jit(solution)/shard_map/dot_general | solution.py:22
  163.0 10.5 %fusion.11 = f32[3,32,2,2,3,1536]{5,1,4,3,2,0:T(8,128)} fusion(bf16[3,32,2,2,3,1536]{5,1,4,3,2,0:T(8,128)(2,1)S(1)} %dot_general.37, bf16[1536,1536,1,1,1,1]{1,0,5,4,3,2:T(8,128)(2,1)} %fusion.138), kind=kOutput, calls=%fused_computation.25 | convolution fusion | flops 5435817984 | bytes 15335424 | tf_op jit(solution)/shard_map/dot_general | solution.py:19
  173.5 6.5 fusion.40
  179.9 2.7 copy.62
  182.7 2.1 gather_fusion
  184.8 11.6 %gather_fusion.1 = f32[48,3,2,3,1536]{4,2,3,1,0:T(2,128)} fusion(f32[3,32,2,3,1536]{4,2,3,1,0:T(2,128)S(1)} %copy.62, s32[1024]{0:T(1024)S(1)} %pad_clamp_fusion), kind=kCustom, calls=%fused_computation.1.clone | custom fusion | bytes 10617024 | tf_op jit(solution)/shard_map/jit(_take)/gather | solution.py:87
  196.5 4.7 copy.67
  201.2 2.1 gather_fusion.2
  203.3 11.4 %gather_fusion.3 = f32[48,3,2,3,1536]{4,2,3,1,0:T(2,128)} fusion(f32[3,32,2,3,1536]{4,2,3,1,0:T(2,128)S(1)} %copy.67, s32[1024]{0:T(1024)S(1)} %pad_clamp_fusion), kind=kCustom, calls=%fused_computation.3.clone | custom fusion | bytes 10617024 | tf_op jit(solution)/shard_map/jit(_take)/gather | solution.py:90
  214.7 1.9 bitcast_multiply_fusion.1
  216.6 0.6 reshape.261
  217.3 0.6 reshape.262
  218.0 11.6 %select_bitcast_fusion.1 = (f32[3,48,2,3,1536]{4,2,3,0,1:T(2,128)}, f32[3,48,2,3,1536]{4,2,3,0,1:T(2,128)}) fusion(f32[48,3,2,3,1536]{4,2,3,1,0:T(2,128)} %gather_fusion.1, pred[48]{0:T(512)(128)(4,1)S(1)} %copy-done.5, f32[48,3,2,3,1536]{4,2,3,1,0:T(2,128)} %gather_fusion.3), kind=kLoop, calls=%fused_computation.21 | loop fusion | flops 2654208 | bytes 21233712 | tf_op jit(solution)/shard_map/jit(_take)/select_n | solution.py:87
  229.6 8.8 %reshape.198 = f32[3,6,8,2,3,4,384]{6,5,3,4,0,2,1:T(4,128)} reshape(f32[3,48,2,3,1536]{4,2,3,0,1:T(2,128)} %get-tuple-element.13) | data formatting | bytes 10616832 | tf_op jit(solution)/shard_map/reshape | solution.py:87
  238.4 5.8 copy.66
  244.2 8.6 %reshape.200 = f32[3,6,8,2,3,4,384]{6,5,3,4,0,2,1:T(4,128)} reshape(f32[3,48,2,3,1536]{4,2,3,0,1:T(2,128)} %get-tuple-element.14) | data formatting | bytes 10616832 | tf_op jit(solution)/shard_map/reshape | solution.py:90
  252.8 3.6 copy.71
  256.4 0.5 copy-done.3
  256.9 9.5 %add_reduce_fusion = (f32[6,8,3,3,3,384]{5,1,4,3,2,0:T(8,128)S(1)}, f32[6,8,3,3,3,384]{5,1,4,3,2,0:T(8,128)S(1)}) fusion(f32[6,8,3,2,3,4,384]{6,1,5,4,3,2,0:T(8,128)S(1)} %copy.71, f32[6,8,3,2,3,4,384]{6,1,5,4,3,2,0:T(8,128)S(1)} %copy-done.3, f32[3,6,2,3,4,384]{5,4,2,3,0,1:T(4,128)S(1)} %reshape.261, f32[3,6,2,3,4,384]{5,4,2,3,0,1:T(4,128)S(1)} %reshape.262), kind=kLoop, calls=%fused_computation.6 | loop fusion | flops 30855168 | bytes 15925248 | tf_op jit(solution)/shard_map/reduce_sum | solution.py:97
  266.4 0.1 copy.72
  266.5 0.1 copy.73
  266.6 0.5 pad_maximum_fusion
  267.1 4.4 copy.74
  271.5 6.8 reshape.201
  278.3 8.0 %dot_general.41 = f32[9,2,3,4,96,48]{4,3,2,1,0,5:T(4,128)} reshape(f32[20736,48]{0,1:T(8,128)} %bitcast.165) | data formatting | bytes 7962624 | tf_op jit(solution)/shard_map/dot_general | solution.py:113
  286.3 7.2 fusion.32
  293.5 16.2 %copy.96 = f32[32,4,3,9,2,3,96]{6,5,4,3,2,1,0:T(4,128)} copy(f32[32,4,3,9,2,3,96]{6,0,1,5,4,3,2:T(8,128)S(1)} %fusion.32) | data formatting | bytes 15925248 | tf_op jit(solution)/shard_map/reshape | solution.py:120
  309.7 22.5 %reshape.263 = f32[128,3,9,2,288]{4,3,2,1,0:T(2,128)} reshape(f32[32,4,3,9,2,3,96]{6,5,4,3,2,1,0:T(4,128)} %copy.96) | data formatting | bytes 15925248 | tf_op jit(solution)/shard_map/reshape | solution.py:120
  332.2 10.2 %all-to-all-start.1 = ((f32[128,3,9,2,288]{4,3,2,1,0:T(2,128)}), f32[128,3,9,2,288]{4,3,2,1,0:T(2,128)}, u32[]{:S(2)}, u32[]{:S(2)}) async-start(f32[128,3,9,2,288]{4,3,2,1,0:T(2,128)} %reshape.263), calls=%async_computation.1 | async-start | bytes 21233664 | tf_op jit(solution)/shard_map/all_to_all | solution.py:121
  342.4 0.0 reduce-scatter.2.cloned.1.call-start
  342.4 131.8 %all-to-all-done.1 = f32[128,3,9,2,288]{4,3,2,1,0:T(2,128)} async-done(((f32[128,3,9,2,288]{4,3,2,1,0:T(2,128)}), f32[128,3,9,2,288]{4,3,2,1,0:T(2,128)}, u32[]{:S(2)}, u32[]{:S(2)}) %all-to-all-start.1) | async-done | bytes 7962656 | tf_op jit(solution)/shard_map/all_to_all | solution.py:121
  474.3 19.1 %copy.97 = f32[128,3,9,2,288]{0,4,2,1,3:T(8,128)} copy(f32[128,3,9,2,288]{4,3,2,1,0:T(2,128)} %all-to-all-done.1) | data formatting | bytes 15925248 | tf_op jit(solution)/shard_map/reshape | solution.py:122
  493.4 14.4 %fusion.37 = f32[3,9,96,384,1]{3,2,4,1,0:T(8,128)S(1)} fusion(f32[128,3,9,2,3,96]{0,5,4,2,1,3:T(8,128)} %bitcast.158, s32[128,3]{0,1:T(4,128)S(1)} %multiply_add_fusion), kind=kOutput, calls=%fused_computation.54 | convolution fusion | flops 4587798528 | bytes 7964160 | tf_op jit(solution)/shard_map/dsqkl,dkz->sqlz/dot_general | solution.py:130
  507.8 13.8 %fusion.35 = f32[3,9,96,384,1]{3,2,4,1,0:T(8,128)} fusion(f32[128,3,9,2,3,96]{0,5,4,2,1,3:T(8,128)S(1)} %bitcast.159, s32[128,3]{0,1:T(4,128)S(1)} %multiply_add_fusion), kind=kOutput, calls=%fused_computation.52 | convolution fusion | flops 4587798528 | bytes 7964672 | tf_op jit(solution)/shard_map/dsqkl,dkz->sqlz/dot_general | solution.py:128
  521.6 10.6 %fusion.38 = f32[3,9,96,384,1]{3,2,4,1,0:T(8,128)S(1)} fusion(f32[128,3,9,2,3,96]{0,5,4,2,1,3:T(8,128)S(1)} %bitcast.160, s32[128,3]{0,1:T(4,128)S(1)} %multiply_add_fusion), kind=kOutput, calls=%fused_computation.55 | convolution fusion | flops 4587798528 | bytes 7964672 | tf_op jit(solution)/shard_map/dsqkl,dkz->sqlz/dot_general | solution.py:127
  532.2 10.7 %fusion.36 = f32[3,9,96,384,1]{3,2,4,1,0:T(8,128)S(1)} fusion(f32[128,3,9,2,3,96]{0,5,4,2,1,3:T(8,128)S(1)} %bitcast.161, s32[128,3]{0,1:T(4,128)S(1)} %multiply_add_fusion), kind=kOutput, calls=%fused_computation.53 | convolution fusion | flops 4587798528 | bytes 7964672 | tf_op jit(solution)/shard_map/dsqkl,dkz->sqlz/dot_general | solution.py:125
  542.9 13.9 %fusion.29 = f32[384,3,9,384]{3,0,2,1:T(8,128)S(1)} fusion(f32[3,9,96,384,1]{3,2,4,1,0:T(8,128)S(1)} %fusion.38, f32[3,9,96,384,1]{3,2,4,1,0:T(8,128)S(1)} %fusion.36, s32[96]{0:T(128)S(1)} %iota_add_fusion), kind=kOutput, calls=%fused_computation.48 | convolution fusion | flops 4587798528 | bytes 23888256 | tf_op jit(solution)/shard_map/ak,sqkz->asqz/dot_general | solution.py:134
  556.8 20.0 %subtract_multiply_fusion = f32[384,3,9,384]{3,0,2,1:T(8,128)} fusion(f32[384,3,9,384]{3,0,2,1:T(8,128)S(1)} %fusion.29, f32[3,9,96,384,1]{3,2,4,1,0:T(8,128)S(1)} %fusion.37, f32[3,9,96,384,1]{3,2,4,1,0:T(8,128)} %fusion.35, s32[96]{0:T(128)S(1)} %iota_add_fusion), kind=kOutput, calls=%fused_computation.4 | convolution fusion | flops 4595761152 | bytes 39813504 | tf_op jit(solution)/shard_map/ak,sqkz->asqz/dot_general | solution.py:135
  576.8 0.0 reduce-scatter.2.cloned.1.call-update
  576.9 141.5 %reduce-scatter.2.cloned.1.call-done = f32[96,3,9,384]{3,0,2,1:T(8,128)} async-done(((f32[384,3,9,384]{3,0,2,1:T(8,128)}), f32[96,3,9,384]{3,0,2,1:T(8,128)}) %reduce-scatter.2.cloned.1.call-update) | async-done | bytes 3981328 | tf_op jit(solution)/shard_map/reduce_scatter | solution.py:136
  718.4 0.0 copy-done.1
  (20 shorter events, 0.1 us)
Async XLA Ops:
  6.5 19.6 %copy-start = (bf16[3,1,384,1536]{3,2,1,0:T(8,128)(2,1)S(1)}, bf16[3,1,384,1536]{3,2,1,0:T(8,128)(2,1)}, u32[]{:S(2)}) copy-start(bf16[3,1,384,1536]{3,2,1,0:T(8,128)(2,1)} %param.8) | copy-start | bytes 10616836
  53.7 11.8 %copy-start.8 = (s32[6]{0:T(128)S(1)}, s32[6]{0:T(128)}, u32[]{:S(2)}) copy-start(s32[6]{0:T(128)} %param.9) | copy-start | bytes 76
  53.7 11.9 %copy-start.7 = (s32[8]{0:T(128)S(1)}, s32[8]{0:T(128)}, u32[]{:S(2)}) copy-start(s32[8]{0:T(128)} %param.10) | copy-start | bytes 100
  53.7 92.5 %all-to-all-start = ((bf16[128,3,1,2,2,3,384]{6,4,5,3,2,1,0:T(2,128)(2,1)}), bf16[128,3,1,2,2,3,384]{6,4,5,3,2,1,0:T(2,128)(2,1)S(1)}, u32[]{:S(2)}, u32[]{:S(2)}) async-start(bf16[128,3,1,2,2,3,384]{6,4,5,3,2,1,0:T(2,128)(2,1)} %copy.60), calls=%async_computation | async-start | bytes 7077888 | tf_op jit(solution)/shard_map/all_to_all | solution.py:62
  67.0 0.5 copy-start.9
  203.3 11.4 %copy-start.6 = (pred[6]{0:T(512)(128)(4,1)S(1)}, pred[6]{0:T(512)(128)(4,1)}, u32[]{:S(2)}) copy-start(pred[6]{0:T(512)(128)(4,1)} %compare_and_fusion.1) | copy-start | bytes 22
  214.7 3.2 copy-start.5
  252.8 4.1 copy-start.3
  278.3 8.0 %copy-start.4 = (s32[48]{0:T(128)S(1)}, s32[48]{0:T(128)}, u32[]{:S(2)}) copy-start(s32[48]{0:T(128)} %multiply_add_fusion.3) | copy-start | bytes 580
  332.2 142.1 %all-to-all-start.1 = ((f32[128,3,9,2,288]{4,3,2,1,0:T(2,128)}), f32[128,3,9,2,288]{4,3,2,1,0:T(2,128)}, u32[]{:S(2)}, u32[]{:S(2)}) async-start(f32[128,3,9,2,288]{4,3,2,1,0:T(2,128)} %reshape.263), calls=%async_computation.1 | async-start | bytes 21233664 | tf_op jit(solution)/shard_map/all_to_all | solution.py:121
  342.4 376.0 %reduce-scatter.2.cloned.1.call-start = ((), (), s32[]{:S(2)}) async-start(), calls=%async_computation.3 | async-start | bytes 19906560 | tf_op jit(solution)/shard_map/reduce_scatter | solution.py:136
  493.4 14.4 %copy-start.2 = (f32[128,3,9,2,288]{0,4,2,1,3:T(8,128)S(1)}, f32[128,3,9,2,288]{0,4,2,1,3:T(8,128)}, u32[]{:S(2)}) copy-start(f32[128,3,9,2,288]{0,4,2,1,3:T(8,128)} %copy.97) | copy-start | bytes 23887876
  576.8 141.5 %copy-start.1 = (bf16[3,1,384,1536]{3,2,1,0:T(8,128)(2,1)S(1)}, bf16[3,1,384,1536]{3,2,1,0:T(8,128)(2,1)}, u32[]{:S(2)}) copy-start(bf16[3,1,384,1536]{3,2,1,0:T(8,128)(2,1)} %param.8) | copy-start | bytes 10616836
Sparse Core Ops, SparseCore 0:
  577.0 141.3 reduce-scatter.1
where the time goes:
time: 736 us; the launch traced here: 726 us
  waiting for transfers between devices  273 us (37%)
  local copies, waits for them, and re-layouts  169 us (23%)
  other arithmetic  130 us (18%)
  matrix products  118 us (16%)
  starting transfers between devices  22 us (3%)
  between operations  14.1 us (2%)
    reduce_scatter x1, waiting for transfers between devices, per_device(): lax.psum_scatter(summed * norm_scale, 'gx', scatter_dimension=0, tiled=True)  141 us
    all_to_all x1, waiting for transfers between devices, per_device(): lax.all_to_all(buffer, ('gy', 'gx'), split_axis=0, concat_axis=0, tiled=T...  132 us
    reshape x2, local copies, waits for them, and re-layouts, per_device(): buffer = placed.reshape(devices, slot_count, 9, 2, block_len * lag_block)  38.7 us
    dot_general x1, other arithmetic, x_transform(): jnp.dot(flat_rows, sin_x, preferred_element_type=jnp.float32)  37 us
    dot_general x1, other arithmetic, x_transform(): jnp.dot(flat_rows, cos_x, preferred_element_type=jnp.float32)  36.7 us
    dot_general x1, matrix products, per_device(): jnp.einsum('ak,sqkz->asqz', sin_local, spanwise_span_imag, precision=high...  20 us
    another operation x1, other arithmetic  19.6 us
    reshape x1, local copies, waits for them, and re-layouts, per_device(): arrived.reshape(devices, arrived.shape[1], 9, 2, block_len, lag_block)  19.1 us
  transfers between devices with their start and end apart: 3, of which 2 were waited for; matrix products, arithmetic and copies ran while one was open for 11% of the time, Pallas kernels for 0%

commit v1 on v0

v1 whole, which is shorter than its diff:
```python
import math

import jax
import jax.numpy as jnp
import numpy as np
from jax import lax
from jax.experimental import pallas as pl
from jax.experimental.pallas import tpu as pltpu
from jax.sharding import Mesh, PartitionSpec as P

NX = 1536
NZ = 1536
LAG = 384
NY = 32
REFS = 6
OFFS = 8
PAIRS = REFS * OFFS
SLOTS = 3
CHIPS = 64
DEVICES = 128
QB = 96
F32 = jnp.float32
BF16 = jnp.bfloat16
VMEM_BYTES = 60 * 1024 * 1024


def modes_of(chip, core):
    out = []
    for k in range(3):
        j = 3 * chip + k
        if core == 0:
            out.append(j)
        else:
            out.append(LAG // 2 if j == 0 else LAG - j)
    return out


def z_table():
    z = np.arange(NZ)
    rows = []
    for gy in range(32):
        for gx in range(4):
            kzs = modes_of((gy // 2) * 4 + gx, gy % 2)
            six = kzs + [k + LAG for k in kzs]
            order = [(0, 0), (0, 1), (0, 2), (0, 3), (0, 4), (0, 5), (1, 4), (1, 5), (1, 0), (1, 1), (1, 2), (1, 3)]
            for part, pos in order:
                angle = 2.0 * math.pi / NZ * ((six[pos] * z) % NZ)
                rows.append(np.cos(angle) if part == 0 else -np.sin(angle))
    return np.stack(rows).astype(np.float32)


def x_table():
    out = np.zeros((4, 2, LAG, 2, 4, 128), np.float64)
    x = np.arange(LAG)[:, None]
    lane = np.arange(QB)[None, :]
    for r in range(4):
        for m in range(4):
            angle = 2.0 * math.pi / NX * ((x * (4 * (lane + QB * m) + r)) % NX)
            out[r, 0, :, 0, m, :QB] = np.cos(angle)
            out[r, 1, :, 0, m, :QB] = np.sin(angle)
            out[r, 0, :, 1, m, :QB] = -np.sin(angle)
            out[r, 1, :, 1, m, :QB] = np.cos(angle)
    return out.reshape(4, 2 * LAG, 1024).astype(np.float32)


def x_lag_table():
    out = np.zeros((2, 4, 128, 4, 128), np.float64)
    lane = np.arange(QB)[:, None]
    col = np.arange(QB)[None, :]
    for r in range(4):
        for g in range(4):
            angle = 2.0 * math.pi / LAG * (((4 * lane + r) * (QB * g + col)) % LAG)
            out[0, r, :QB, g, :QB] = np.cos(angle)
            out[1, r, :QB, g, :QB] = -np.sin(angle)
    return out.reshape(1024, 512).astype(np.float32)


def z_lag_table():
    out = np.zeros((CHIPS, 8, LAG), np.float64)
    t = np.arange(LAG)
    for chip in range(CHIPS):
        for k in range(3):
            j = 3 * chip + k
            if j == 0:
                out[chip, k] = (1.0 + (-1.0) ** t) / 2.0
                out[chip, 3 + k] = (1.0 - (-1.0) ** t) / 2.0
            else:
                angle = 2.0 * math.pi / LAG * ((j * t) % LAG)
                out[chip, k] = np.cos(angle)
                out[chip, 3 + k] = -np.sin(angle)
    return out.reshape(CHIPS * 8, LAG).astype(np.float32)


def z_kernel(table_ref, vel_ref, out_ref):
    dests = out_ref.shape[0]
    for c in range(3):
        acc = lax.dot_general(
            table_ref[...], vel_ref[c], (((1,), (1,)), ((), ())), preferred_element_type=F32
        )
        for d in range(dests):
            for t in range(3):
                row = 12 * d + 4 * t
                out_ref[d, t, :, c * LAG : (c + 1) * LAG] = acc[row : row + 4].astype(BF16)


def z_transform(table, vel):
    block = 16
    return pl.pallas_call(
        z_kernel,
        grid=(DEVICES // block,),
        in_specs=[
            pl.BlockSpec((12 * block, NZ), lambda i: (i, 0)),
            pl.BlockSpec((3, LAG, NZ), lambda i: (0, 0, 0)),
        ],
        out_specs=pl.BlockSpec((block, 3, 4, 3 * LAG), lambda i: (i, 0, 0, 0)),
        out_shape=jax.ShapeDtypeStruct((DEVICES, 3, 4, 3 * LAG), BF16),
        compiler_params=pltpu.CompilerParams(vmem_limit_bytes=VMEM_BYTES),
        name="z_transform",
    )(table, vel)


def mid_kernel(
    planes_ref, order_ref, arr_ref, wx_ref, tx_ref, coef_ref, send_ref, keep_ref, lhs_ref, u_ref, prod_ref, res_ref
):
    def butterfly(i, carry):
        pieces = [[] for _ in range(4)]
        for yy in range(2):
            for c in range(3):
                re, im = [], []
                for g in range(4):
                    src = (2 * i + yy) * 4 + g
                    lanes = slice(c * LAG, (c + 1) * LAG)
                    t0 = arr_ref[src, 0, :, lanes].astype(F32)
                    t1 = arr_ref[src, 1, :, lanes].astype(F32)
                    t2 = arr_ref[src, 2, :, lanes].astype(F32)
                    re.append(jnp.concatenate([t0, t1], axis=0))
                    im.append(jnp.concatenate([t2, t1[2:4], t1[0:2]], axis=0))
                s02r, d02r = re[0] + re[2], re[0] - re[2]
                s02i, d02i = im[0] + im[2], im[0] - im[2]
                s13r, d13r = re[1] + re[3], re[1] - re[3]
                s13i, d13i = im[1] + im[3], im[1] - im[3]
                parts = [
                    (s02r + s13r, s02i + s13i),
                    (d02r + d13i, d02i - d13r),
                    (s02r - s13r, s02i - s13i),
                    (d02r - d13i, d02i + d13r),
                ]
                for r in range(4):
                    pieces[r].append(parts[r])
        for r in range(4):
            for h in range(3):
                lo, hi = pieces[r][2 * h], pieces[r][2 * h + 1]
                row = pl.multiple_of(i * 48 + 16 * h, 16)
                for part in range(2):
                    both = jnp.concatenate([lo[part], hi[part]], axis=0).astype(BF16)
                    lhs_ref[r, pl.ds(row, 16), part * LAG : (part + 1) * LAG] = both
        return carry

    lax.fori_loop(0, NY // 2, butterfly, 0)

    def transform(r, carry):
        for tile in range(4):
            out = jnp.dot(
                lhs_ref[r], wx_ref[r, :, tile * 256 : (tile + 1) * 256], preferred_element_type=F32
            )
            u_ref[r, 2 * tile] = out[:, :128].reshape(3 * NY, 8, 128)
            u_ref[r, 2 * tile + 1] = out[:, 128:].reshape(3 * NY, 8, 128)
        return carry

    lax.fori_loop(0, 4, transform, 0)

    alpha = coef_ref[0]
    beta = coef_ref[1]
    weight = coef_ref[2]
    low = lax.broadcasted_iota(jnp.int32, (8, 128), 0) < 3

    def fold(x):
        x = x * weight
        return x + jnp.where(low, pltpu.roll(x, 5, 0), pltpu.roll(x, 3, 0))

    def ref_group(ref, carry):
        first = planes_ref[ref] * 3

        def pair_products(o, inner):
            second = (planes_ref[ref] + planes_ref[REFS + o]) * 3
            for r in range(4):
                acc_re = [None] * 9
                acc_im = [None] * 9
                for m in range(4):
                    ar = [u_ref[r, m, first + i] for i in range(3)]
                    ai = [u_ref[r, 4 + m, first + i] for i in range(3)]
                    br = [u_ref[r, m, second + j] for j in range(3)]
                    bi = [u_ref[r, 4 + m, second + j] for j in range(3)]
                    for i in range(3):
                        for j in range(3):
                            re = ar[i] * br[j] + ai[i] * bi[j]
                            im = ar[i] * bi[j] - ai[i] * br[j]
                            ij = 3 * i + j
                            acc_re[ij] = re if m == 0 else acc_re[ij] + re
                            acc_im[ij] = im if m == 0 else acc_im[ij] + im
                for ij in range(9):
                    re = fold(acc_re[ij])
                    im = fold(acc_im[ij])
                    row = o * 9 + ij
                    prod_ref[row, :, r * 128 : (r + 1) * 128] = alpha * re + beta * im
                    prod_ref[row, :, 512 + r * 128 : 512 + (r + 1) * 128] = alpha * im - beta * re
            return inner

        lax.fori_loop(0, OFFS, pair_products, 0)
        lhs = prod_ref[...].reshape(OFFS * 72, 1024).astype(BF16)
        out = jnp.dot(lhs, tx_ref[...], preferred_element_type=F32)
        res_ref[pl.ds(ref * 72, 72)] = out.reshape(OFFS * 9, 8, 512)
        return carry

    lax.fori_loop(0, REFS, ref_group, 0)
    res_ref[pl.ds(PAIRS * 9, 9)] = jnp.zeros((9, 8, 512), F32)

    lane = lax.broadcasted_iota(jnp.int32, (8, 128), 1)

    def pack(base, out_ref):
        def owner(o, carry):
            at = [order_ref[base + o * SLOTS + s] * 9 for s in range(SLOTS)]
            for g in range(4):
                for group in range(7):
                    count = 4 if group < 6 else 3
                    piece = []
                    for n in range(count):
                        f = 4 * group + n
                        v = res_ref[at[f // 9] + f % 9, :, g * 128 : (g + 1) * 128]
                        piece.append(pltpu.roll(v, 96 * n % 128, 1) if n else v)
                    v0 = jnp.where(lane < 96, piece[0], piece[1])
                    v1 = jnp.where(lane < 64, piece[1], piece[2])
                    if count == 4:
                        v2 = jnp.where(lane < 32, piece[2], piece[3])
                    else:
                        v2 = jnp.where(lane < 32, piece[2], 0.0)
                    wide = jnp.concatenate([v0, v1, v2], axis=1).astype(BF16)
                    out_ref[o, g, :, group * 384 : (group + 1) * 384] = wide
            return carry

        lax.fori_loop(0, 16, owner, 0)

    pack(0, send_ref)
    pack(16 * SLOTS, keep_ref)


def middle(planes, order, arr, wx, tx, coef):
    shape = jax.ShapeDtypeStruct((16, 4, 8, 2688), BF16)
    vmem = pl.BlockSpec(memory_space=pltpu.VMEM)
    smem = pl.BlockSpec(memory_space=pltpu.SMEM)
    return pl.pallas_call(
        mid_kernel,
        in_specs=[smem, smem, vmem, vmem, vmem, vmem],
        out_specs=[vmem, vmem],
        out_shape=[shape, shape],
        scratch_shapes=[
            pltpu.VMEM((4, 24 * NY, 2 * LAG), BF16),
            pltpu.VMEM((4, 8, 3 * NY, 8, 128), F32),
            pltpu.VMEM((OFFS * 9, 8, 1024), F32),
            pltpu.VMEM(((PAIRS + 1) * 9, 8, 512), F32),
        ],
        compiler_params=pltpu.CompilerParams(vmem_limit_bytes=VMEM_BYTES),
        name="middle",
    )(planes, order, arr, wx, tx, coef)


def lag_kernel(x_ref, hi_ref, lo_ref, out_ref):
    dims = (((0,), (0,)), ((), ()))
    x = x_ref[...]
    acc = lax.dot_general(x, hi_ref[...], dims, preferred_element_type=F32)
    acc = acc + lax.dot_general(x, lo_ref[...], dims, preferred_element_type=F32)
    out_ref[...] = acc * (2.0 / float(NX * NZ) ** 2)


def z_lags(x, hi, lo):
    return pl.pallas_call(
        lag_kernel,
        grid=(7,),
        in_specs=[
            pl.BlockSpec((CHIPS * 8, 384), lambda i: (0, i)),
            pl.BlockSpec((CHIPS * 8, LAG), lambda i: (0, 0)),
            pl.BlockSpec((CHIPS * 8, LAG), lambda i: (0, 0)),
        ],
        out_specs=pl.BlockSpec((384, LAG), lambda i: (i, 0)),
        out_shape=jax.ShapeDtypeStruct((SLOTS * 9 * QB, LAG), F32),
        compiler_params=pltpu.CompilerParams(vmem_limit_bytes=VMEM_BYTES),
        name="z_lags",
    )(x, hi, lo)


def per_device(velocity, ref_planes, partner_offsets, band_owner):
    core = lax.axis_index("core")
    first_chip = (lax.axis_index("y") == 0) & (lax.axis_index("x") == 0) & (lax.axis_index("z") == 0)

    forward_z = jnp.asarray(z_table()).astype(BF16)
    parcels = z_transform(forward_z, velocity.reshape(3, LAG, NZ))
    arrived = lax.all_to_all(parcels, ("y", "x", "core", "z"), split_axis=0, concat_axis=0, tiled=True)

    pair = jnp.arange(PAIRS, dtype=jnp.int32)
    same = band_owner[:, None] == band_owner[None, :]
    slot = jnp.sum((same & (pair[None, :] < pair[:, None])).astype(jnp.int32), axis=1)
    dest = band_owner * SLOTS + slot
    hit = dest[None, :] == jnp.arange(32 * SLOTS, dtype=jnp.int32)[:, None]
    table = PAIRS + jnp.sum(jnp.where(hit, pair[None, :] - PAIRS, 0), axis=1)
    table = table.reshape(16, 2, SLOTS)
    order = jnp.where(
        core == 0,
        jnp.concatenate([table[:, 1], table[:, 0]]),
        jnp.concatenate([table[:, 0], table[:, 1]]),
    ).reshape(-1)

    row = jnp.arange(8, dtype=jnp.int32)
    sign = jnp.where(core == 0, 1.0, -1.0)
    special = first_chip & (row == 3)
    odd = row >= 3
    alpha = jnp.where(odd, jnp.where(special, sign, 0.0), 1.0)
    beta = jnp.where(odd & ~special, sign, 0.0)
    weight = jnp.where(first_chip & (core == 0) & (row == 0), 0.5, 1.0)
    coef = jnp.broadcast_to(jnp.stack([alpha, beta, weight])[:, :, None], (3, 8, 128)).astype(F32)

    send, keep = middle(
        jnp.concatenate([ref_planes, partner_offsets]),
        order,
        arrived,
        jnp.asarray(x_table()).astype(BF16),
        jnp.asarray(x_lag_table()).astype(BF16),
        coef,
    )
    other = lax.ppermute(send, "core", [(0, 1), (1, 0)])
    folded = (keep.astype(F32) + other.astype(F32)).astype(BF16).reshape(CHIPS, 8, 2688)
    spread = lax.all_to_all(folded, ("y", "x", "z"), split_axis=0, concat_axis=0, tiled=True)
    full = jnp.asarray(z_lag_table())
    hi = full.astype(BF16)
    lo = (full - hi.astype(F32)).astype(BF16)
    lags = z_lags(spread.reshape(CHIPS * 8, 2688), hi, lo)
    return lags.reshape(SLOTS, 9, QB, LAG)


def solution(mesh):
    inner = Mesh(mesh.devices.reshape(4, 4, 2, 4), ("y", "x", "core", "z"))
    gy = ("y", "x", "core")
    return jax.shard_map(
        per_device,
        mesh=inner,
        in_specs=(P(None, gy, "z", None), P(), P(), P()),
        out_specs=P(gy, None, "z", None),
        check_vma=False,
    )
```

time: 736 us -> 165 us (0.22); the launches traced: 726 us -> 164 us
  waiting for transfers between devices: 273 us -> 44.3 us
  local copies, waits for them, and re-layouts: 169 us -> 6.12 us
  other arithmetic: 130 us -> 5.17 us
  matrix products: 118 us -> 0 us
  Pallas kernels: 0 us -> 55.5 us
  blocking collectives: 0 us -> 41.1 us
  between operations: 14.1 us -> 0.06 us
  starting transfers between devices: 22 us -> 11.5 us
    reduce_scatter x1 -> x0, waiting for transfers between devices: 141 us -> none  [per_device(): lax.psum_scatter(summed * norm_scale, 'gx', scatter_dimension=0, tiled=True)]
    dot_general x10 -> x0, matrix products: 118 us -> none  [the longest x1 20 us: per_device(): jnp.einsum('ak,sqkz->asqz', sin_local, spanwise_span_imag, precision=high...]
    all_to_all x2 -> x1, waiting for transfers between devices: 132 us -> 39 us  [per_device(): lax.all_to_all(parcels, ('y', 'x', 'core', 'z'), split_axis=0, concat_axi...]
    reshape x9 -> x0, local copies, waits for them, and re-layouts: 86.9 us -> none  [the longest x2 38.7 us: per_device(): buffer = placed.reshape(devices, slot_count, 9, 2, block_len * lag_block)]
    dot_general x2 -> x0, other arithmetic: 73.6 us -> none  [the longest x1 37 us: x_transform(): jnp.dot(flat_rows, sin_x, preferred_element_type=jnp.float32)]
    pallas_call x0 -> x3, Pallas kernels: none -> 55.5 us  [the longest x1 33.9 us: middle(): pl.pallas_call(mid_kernel, in_specs=[smem, smem, vmem, vmem, vmem, vmem],...]
    all_to_all x0 -> x1, blocking collectives: none -> 41.1 us  [per_device(): lax.all_to_all(folded, ('y', 'x', 'z'), split_axis=0, concat_axis=0, tile...]
    gather x4 -> x0, local copies, waits for them, and re-layouts: 27.3 us -> none  [the longest x1 11.6 us: per_device(): jnp.take(real_part, partner_index, axis=1)]
  transfers between devices with their start and end apart: 3 -> 2, of which waited for: 2 -> 2; matrix products, arithmetic and copies ran while one was open for 11% -> 4% of each run, Pallas kernels for 0% -> 0%
where the time goes in v1:
time: 165 us; the launch traced here: 164 us
  Pallas kernels  55.5 us (34%)
  waiting for transfers between devices  44.3 us (27%)
  blocking collectives  41.1 us (25%)
  starting transfers between devices  11.5 us (7%)
  local copies, waits for them, and re-layouts  6.12 us (4%)
  other arithmetic  5.17 us (3%)
    all_to_all x1, blocking collectives, per_device(): lax.all_to_all(folded, ('y', 'x', 'z'), split_axis=0, concat_axis=0, tile...  41.1 us
    all_to_all x1, waiting for transfers between devices, per_device(): lax.all_to_all(parcels, ('y', 'x', 'core', 'z'), split_axis=0, concat_axi...  39 us
    pallas_call x1, Pallas kernels, middle(): pl.pallas_call(mid_kernel, in_specs=[smem, smem, vmem, vmem, vmem, vmem],...  33.9 us
    pallas_call x1, Pallas kernels, z_transform(): pl.pallas_call(z_kernel, grid=(DEVICES // block,), in_specs=[pl.BlockSpec...  13.4 us
    all_to_all x1, starting transfers between devices, per_device(): lax.all_to_all(parcels, ('y', 'x', 'core', 'z'), split_axis=0, concat_axi...  11.5 us
    pallas_call x1, Pallas kernels, z_lags(): pl.pallas_call(lag_kernel, grid=(7,), in_specs=[pl.BlockSpec((CHIPS * 8,...  8.1 us
    ppermute x1, waiting for transfers between devices, per_device(): other = lax.ppermute(send, 'core', [(0, 1), (1, 0)])  5.3 us
  transfers between devices with their start and end apart: 2, of which 2 were waited for; matrix products, arithmetic and copies ran while one was open for 4% of the time, Pallas kernels for 0%

profile of v1, /device:TPU:1, one launch (start us, length us, event | category | flops | bytes accessed | tf_op | source)
XLA Modules:
  0.0 163.7 jit_solution(2630879641323437703)
XLA Ops:
  0.0 13.4 %z_transform.1 = bf16[128,3,4,1152]{3,2,1,0:T(4,128)(2,1)} custom-call(bf16[1536,1536]{1,0:T(8,128)(2,1)} %constant.48.table_ref, bf16[3,384,1536]{2,1,0:T(8,128)(2,1)} %bitcast.8), custom_call_target="tpu_custom_call" | custom-call | tf_op jit(solution)/shard_map/z_transform/pallas_call | solution.py:108
  13.4 0.0 copy-start.1
  13.5 11.5 %all-to-all-start = ((bf16[128,3,4,1152]{3,2,1,0:T(4,128)(2,1)}), bf16[128,3,4,1152]{3,2,1,0:T(4,128)(2,1)S(1)}, u32[]{:S(2)}, u32[]{:S(2)}) async-start(bf16[128,3,4,1152]{3,2,1,0:T(4,128)(2,1)} %z_transform.1), calls=%async_computation | async-start | bytes 7077888 | tf_op jit(solution)/shard_map/all_to_all | solution.py:297
  25.0 0.0 copy-done.1
  25.0 0.2 convert_reduce_fusion
  25.2 0.1 select_reduce_fusion
  25.3 0.6 broadcast_add_fusion
  25.8 0.7 add.25
  26.6 0.6 fusion.1
  27.2 0.8 copy.15
  28.0 0.8 copy.16
  28.7 0.6 add_select_fusion
  29.4 0.7 copy.17
  30.1 0.7 select_n.66.order_ref
  30.8 1.3 pad_add_fusion.planes_ref
  32.1 39.0 %all-to-all-done.arr_ref = bf16[128,3,4,1152]{3,2,1,0:T(4,128)(2,1)S(1)} async-done(((bf16[128,3,4,1152]{3,2,1,0:T(4,128)(2,1)}), bf16[128,3,4,1152]{3,2,1,0:T(4,128)(2,1)S(1)}, u32[]{:S(2)}, u32[]{:S(2)}) %all-to-all-start) | async-done | bytes 3538976 | tf_op jit(solution)/shard_map/all_to_all | solution.py:297
  71.1 0.0 copy-start
  71.1 0.8 broadcast_in_dim.51.coef_ref
  71.9 1.0 copy-done
  72.9 33.9 %middle.1 = (bf16[16,4,8,2688]{3,2,1,0:T(8,128)(2,1)}, bf16[16,4,8,2688]{3,2,1,0:T(8,128)(2,1)}) custom-call(s32[14]{0:T(128)} %pad_add_fusion.planes_ref, s32[96]{0:T(128)} %select_n.66.order_ref, bf16[128,3,4,1152]{3,2,1,0:T(4,128)(2,1)} %copy-done, bf16[4,768,1024]{2,1,0:T(8,128)(2,1)} %constant.49.wx_ref, bf16[1024,512]{1,0:T(8,128)(2,1)} %constant.50.tx_ref, ...), custom_call_target="tpu_custom_call" | custom-call | tf_op jit(solution)/shard_map/middle/pallas_call | solution.py:251
  106.8 0.0 collective-permute-start
  106.8 5.3 %collective-permute-done = bf16[16,4,8,2688]{3,2,1,0:T(8,128)(2,1)S(1)} collective-permute-done((bf16[16,4,8,2688]{3,2,1,0:T(8,128)(2,1)}, bf16[16,4,8,2688]{3,2,1,0:T(8,128)(2,1)S(1)}, u32[]{:S(2)}, u32[]{:S(2)}) %collective-permute-start) | collective-permute-done | bytes 2752544 | tf_op jit(solution)/shard_map/ppermute | solution.py:329
  112.1 2.4 %add_convert_fusion = bf16[16,4,8,2688]{3,2,1,0:T(8,128)(2,1)S(1)} fusion(bf16[16,4,8,2688]{3,2,1,0:T(8,128)(2,1)S(1)} %collective-permute-done, bf16[16,4,8,2688]{3,2,1,0:T(8,128)(2,1)} %get-tuple-element.7), kind=kLoop, calls=%fused_computation | loop fusion | flops 5505024 | bytes 8257536 | tf_op jit(solution)/shard_map/convert_element_type | solution.py:330
  114.6 41.1 %all_to_all.10 = bf16[64,8,2688]{2,1,0:T(8,128)(2,1)} all-to-all(bf16[64,8,2688]{2,1,0:T(8,128)(2,1)S(1)} %bitcast.7), channel_id=1, replica_groups=mesh['y'=4,'x'=4,'core'=2,'z'=4] {'y','x','z'}, dimensions={0} | all-to-all | bytes 5505024 | tf_op jit(solution)/shard_map/all_to_all | solution.py:331
  155.6 8.1 %z_lags.1 = f32[2592,384]{1,0:T(8,128)} custom-call(bf16[512,2688]{1,0:T(8,128)(2,1)} %bitcast.6, bf16[512,384]{1,0:T(8,128)(2,1)} %constant.51.hi_ref, bf16[512,384]{1,0:T(8,128)(2,1)} %constant.54.lo_ref), custom_call_target="tpu_custom_call" | custom-call | tf_op jit(solution)/shard_map/z_lags/pallas_call | solution.py:276
  (4 shorter events, 0.0 us)
Async XLA Ops:
  13.4 11.5 %copy-start.1 = (s32[48]{0:T(128)S(1)}, s32[48]{0:T(128)}, u32[]{:S(2)}) copy-start(s32[48]{0:T(128)} %param.11) | copy-start | bytes 580
  13.5 57.7 %all-to-all-start = ((bf16[128,3,4,1152]{3,2,1,0:T(4,128)(2,1)}), bf16[128,3,4,1152]{3,2,1,0:T(4,128)(2,1)S(1)}, u32[]{:S(2)}, u32[]{:S(2)}) async-start(bf16[128,3,4,1152]{3,2,1,0:T(4,128)(2,1)} %z_transform.1), calls=%async_computation | async-start | bytes 7077888 | tf_op jit(solution)/shard_map/all_to_all | solution.py:297
  71.1 1.8 %copy-start = (bf16[128,3,4,1152]{3,2,1,0:T(4,128)(2,1)}, bf16[128,3,4,1152]{3,2,1,0:T(4,128)(2,1)S(1)}, u32[]{:S(2)}) copy-start(bf16[128,3,4,1152]{3,2,1,0:T(4,128)(2,1)S(1)} %all-to-all-done.arr_ref) | copy-start | bytes 10616836
  106.8 5.3 %collective-permute-start = (bf16[16,4,8,2688]{3,2,1,0:T(8,128)(2,1)}, bf16[16,4,8,2688]{3,2,1,0:T(8,128)(2,1)S(1)}, u32[]{:S(2)}, u32[]{:S(2)}) collective-permute-start(bf16[16,4,8,2688]{3,2,1,0:T(8,128)(2,1)} %get-tuple-element.8), channel_id=1, source_target_pairs={{0,4},{4,0},{1,5},{5,1},{2,6},{6,2},{3,7},{7,3},{8,12},{12,8},{9,1... | collective-permute-start | bytes 8257544 | tf_op jit(solution)/shard_map/ppermute | solution.py:329

commit v2 on v1

v2 whole, which is shorter than its diff:
```python
import math

import jax
import jax.numpy as jnp
import numpy as np
from jax import lax
from jax.experimental import pallas as pl
from jax.experimental.pallas import tpu as pltpu
from jax.sharding import Mesh, PartitionSpec as P

NX = 1536
NZ = 1536
LAG = 384
NY = 32
REFS = 6
OFFS = 8
PAIRS = REFS * OFFS
SLOTS = 3
CHIPS = 64
DEVICES = 128
QB = 96
F32 = jnp.float32
BF16 = jnp.bfloat16
WIDE = 1408
VMEM_BYTES = 60 * 1024 * 1024


def modes_of(chip, core):
    out = []
    for k in range(3):
        j = 3 * chip + k
        if core == 0:
            out.append(j)
        else:
            out.append(LAG // 2 if j == 0 else LAG - j)
    return out


def z_table():
    z = np.arange(NZ)
    order = [(0, 0), (0, 1), (0, 2), (1, 3), (0, 3), (0, 4), (0, 5), (1, 4), (1, 0), (1, 1), (1, 2), (1, 5)]
    rows = []
    for gy in range(32):
        for gx in range(4):
            core = gy % 2
            kzs = modes_of((gy // 2) * 4 + gx, core)
            six = kzs + [k + LAG for k in kzs]
            sign = 1.0 if core == 0 else -1.0
            for part, pos in order:
                angle = 2.0 * math.pi / NZ * ((six[pos] * z) % NZ)
                rows.append(np.cos(angle) if part == 0 else -sign * np.sin(angle))
    return np.stack(rows).astype(np.float32)


def x_table():
    out = np.zeros((4, 2, LAG, 2, 4, 128), np.float64)
    x = np.arange(LAG)[:, None]
    lane = np.arange(QB)[None, :]
    for r in range(4):
        for m in range(4):
            angle = 2.0 * math.pi / NX * ((x * (4 * (lane + QB * m) + r)) % NX)
            out[r, 0, :, 0, m, :QB] = np.cos(angle)
            out[r, 1, :, 0, m, :QB] = np.sin(angle)
            out[r, 0, :, 1, m, :QB] = -np.sin(angle)
            out[r, 1, :, 1, m, :QB] = np.cos(angle)
    return out.reshape(4, 2 * LAG, 4, 256).transpose(2, 0, 1, 3).astype(np.float32)


def x_lag_table():
    out = np.zeros((2, 4, QB, 4, 128), np.float64)
    q = np.arange(QB)[:, None]
    col = np.arange(QB)[None, :]
    for r in range(4):
        for g in range(4):
            angle = 2.0 * math.pi / LAG * (((4 * q + r) * (QB * g + col)) % LAG)
            out[0, r, :, g, :QB] = np.cos(angle)
            out[1, r, :, g, :QB] = -np.sin(angle)
    return out.reshape(2 * LAG, 512).astype(np.float32)


def z_lag_table():
    out = np.zeros((CHIPS, 6, LAG), np.float64)
    t = np.arange(LAG)
    for chip in range(CHIPS):
        for k in range(3):
            j = 3 * chip + k
            if j == 0:
                out[chip, k] = (1.0 + (-1.0) ** t) / 2.0
                out[chip, 3 + k] = (1.0 - (-1.0) ** t) / 2.0
            else:
                angle = 2.0 * math.pi / LAG * ((j * t) % LAG)
                out[chip, k] = np.cos(angle)
                out[chip, 3 + k] = -np.sin(angle)
    return out.reshape(CHIPS * 6, LAG).astype(np.float32)


def z_kernel(table_ref, vel_ref, out_ref):
    half = NZ // 2
    for part in range(2):
        acc = lax.dot_general(
            table_ref[part * half : (part + 1) * half],
            vel_ref[0],
            (((1,), (1,)), ((), ())),
            preferred_element_type=F32,
        )
        for d in range(DEVICES // 2):
            for t in range(3):
                row = 12 * d + 4 * t
                out_ref[part * (DEVICES // 2) + d, 0, t] = acc[row : row + 4].astype(BF16)


def z_transform(table, vel):
    return pl.pallas_call(
        z_kernel,
        grid=(3,),
        in_specs=[
            pl.BlockSpec((NZ, NZ), lambda c: (0, 0)),
            pl.BlockSpec((1, LAG, NZ), lambda c: (c, 0, 0)),
        ],
        out_specs=pl.BlockSpec((DEVICES, 1, 3, 4, LAG), lambda c: (0, c, 0, 0, 0)),
        out_shape=jax.ShapeDtypeStruct((DEVICES, 3, 3, 4, LAG), BF16),
        compiler_params=pltpu.CompilerParams(vmem_limit_bytes=VMEM_BYTES),
        name="z_transform",
    )(table, vel)


def side_by_side(pieces, lane):
    rolled = [pltpu.roll(v, 96 * n % 128, 1) if n else v for n, v in enumerate(pieces)]
    out = [jnp.where(lane < 96, rolled[0], rolled[1])]
    if len(pieces) == 2:
        return out + [jnp.where(lane < 64, rolled[1], 0.0)]
    out.append(jnp.where(lane < 64, rolled[1], rolled[2]))
    out.append(jnp.where(lane < 32, rolled[2], rolled[3]))
    return out


def product_kernel(planes_ref, arr_ref, wx_ref, coef_ref, send_ref, keep_ref, lhs_ref, tmp_ref, u_ref):
    core = planes_ref[REFS + OFFS]
    scale = coef_ref[...]

    def butterfly(i, carry):
        pieces = [[] for _ in range(4)]
        for yy in range(2):
            for c in range(3):
                comp = jnp.where(core == 0, c, 2 - c)
                re, im = [], []
                for g in range(4):
                    src = (2 * i + yy) * 4 + g
                    t0 = arr_ref[src, comp, 0].astype(F32)
                    t1 = arr_ref[src, comp, 1].astype(F32)
                    t2 = arr_ref[src, comp, 2].astype(F32)
                    re.append(jnp.concatenate([t0[0:3], t0[0:1], t1[0:3], t1[0:1]], axis=0))
                    im.append(
                        jnp.concatenate([t2[0:3], t2[0:1], t0[3:4], t1[3:4], t2[3:4], t0[3:4]], axis=0)
                    )
                s02r, d02r = re[0] + re[2], re[0] - re[2]
                s02i, d02i = im[0] + im[2], im[0] - im[2]
                s13r, d13r = re[1] + re[3], re[1] - re[3]
                s13i, d13i = im[1] + im[3], im[1] - im[3]
                parts = [
                    (s02r + s13r, s02i + s13i),
                    (d02r + d13i, d02i - d13r),
                    (s02r - s13r, s02i - s13i),
                    (d02r - d13i, d02i + d13r),
                ]
                for r in range(4):
                    pieces[r].append([part * scale for part in parts[r]])
        for r in range(4):
            for h in range(3):
                lo, hi = pieces[r][2 * h], pieces[r][2 * h + 1]
                row = pl.multiple_of(i * 48 + 16 * h, 16)
                for part in range(2):
                    both = jnp.concatenate([lo[part], hi[part]], axis=0).astype(BF16)
                    lhs_ref[r, pl.ds(row, 16), part * LAG : (part + 1) * LAG] = both
        return carry

    lax.fori_loop(0, NY // 2, butterfly, 0)

    lane = lax.broadcasted_iota(jnp.int32, (8, 128), 1)

    def transform(tile, carry):
        for r in range(4):
            out = jnp.dot(lhs_ref[r], wx_ref[tile, r], preferred_element_type=F32)
            tmp_ref[r] = out.reshape(3 * NY, 8, 256)

        def merge(n, inner):
            for k in range(4):
                row = 4 * n + k
                for h in range(2):
                    v = side_by_side([tmp_ref[r, row, :, h * 128 : (h + 1) * 128] for r in range(4)], lane)
                    u_ref[2 * tile + h, row] = jnp.concatenate(v, axis=1)
            return inner

        lax.fori_loop(0, 3 * NY // 4, merge, 0)
        return carry

    lax.fori_loop(0, 4, transform, 0)

    low = lax.broadcasted_iota(jnp.int32, (8, 128), 0) < 4

    def pair_products(p, carry):
        plane = planes_ref[p // OFFS]
        first = plane * 3
        second = (plane + planes_ref[REFS + p % OFFS]) * 3
        for lg in range(3):
            at = slice(lg * 128, (lg + 1) * 128)
            sums = [None] * 27
            for m in range(4):
                ar = [u_ref[m, first + i, :, at] for i in range(3)]
                ai = [u_ref[4 + m, first + i, :, at] for i in range(3)]
                br = [u_ref[m, second + j, :, at] for j in range(3)]
                bi = [u_ref[4 + m, second + j, :, at] for j in range(3)]
                ad = [ar[i] - ai[i] for i in range(3)]
                bs = [br[j] + bi[j] for j in range(3)]
                for i in range(3):
                    for j in range(3):
                        n = 3 * (3 * i + j)
                        for q, term in enumerate((ar[i] * br[j], ai[i] * bi[j], ad[i] * bs[j])):
                            sums[n + q] = term if m == 0 else sums[n + q] + term
            for ij in range(9):
                rr, ii, mixed = sums[3 * ij : 3 * ij + 3]
                re = rr + ii
                im = mixed + (ii - rr)
                folded = jnp.where(low, re, im) + pltpu.roll(jnp.where(low, im, re), 4, 0)
                if ij <= 4:
                    keep_ref[p, ij, :, at] = folded
                if ij >= 4:
                    send_ref[p, 8 - ij, :, at] = folded
        return carry

    lax.fori_loop(0, PAIRS, pair_products, 0)


def products(planes, arr, wx, coef):
    shape = jax.ShapeDtypeStruct((PAIRS, 5, 8, LAG), F32)
    vmem = pl.BlockSpec(memory_space=pltpu.VMEM)
    smem = pl.BlockSpec(memory_space=pltpu.SMEM)
    return pl.pallas_call(
        product_kernel,
        in_specs=[smem, vmem, vmem, vmem],
        out_specs=[vmem, vmem],
        out_shape=[shape, shape],
        scratch_shapes=[
            pltpu.VMEM((4, 24 * NY, 2 * LAG), BF16),
            pltpu.VMEM((4, 3 * NY, 8, 256), F32),
            pltpu.VMEM((8, 3 * NY, 8, LAG), F32),
        ],
        compiler_params=pltpu.CompilerParams(vmem_limit_bytes=VMEM_BYTES),
        name="products",
    )(planes, arr, wx, coef)


def x_lag_kernel(order_ref, keep_ref, other_ref, tx_ref, coef_ref, out_ref, res_ref):
    ref = pl.program_id(0)
    total = keep_ref[...] * coef_ref[0] + other_ref[...] * coef_ref[1]
    total = total.reshape(OFFS * 5 * 8, LAG)
    swap = coef_ref[2] > 0.5
    sign = coef_ref[3]
    rows = OFFS * 5
    halves = [[], []]
    for n in range(rows):
        x = total[8 * n : 8 * n + 8]
        halves[0].append(jnp.where(swap, pltpu.roll(x, 1, 0), x))
        halves[1].append(jnp.where(swap, pltpu.roll(x, 5, 0), pltpu.roll(x, 4, 0) * sign))
    lhs = jnp.concatenate([jnp.concatenate(h, axis=0) for h in halves], axis=1).astype(BF16)
    out = jnp.dot(lhs, tx_ref[...], preferred_element_type=F32)
    low = lax.broadcasted_iota(jnp.int32, (8, 512), 0) < 3
    for n in range(rows):
        x = out[8 * n : 8 * n + 8]
        res_ref[ref * rows + n] = jnp.where(low, x, pltpu.roll(x, 7, 0))

    @pl.when(ref == REFS - 1)
    def _():
        res_ref[PAIRS * 5 : PAIRS * 5 + 5] = jnp.zeros((5, 8, 512), F32)
        core = order_ref[32 * SLOTS]
        lane = lax.broadcasted_iota(jnp.int32, (8, 128), 1)

        def owner(o, carry):
            at = [order_ref[o * SLOTS + s] * 5 for s in range(SLOTS)]
            index = [at[f // 4] + f % 4 for f in range(12)]
            index.append(jnp.where(core == 0, at[0], at[1]) + 4)
            index.append(jnp.where(core == 0, at[2] + 4, PAIRS * 5))
            for g in range(4):
                for group in range(4):
                    pick = index[4 * group : 4 * group + 4]
                    v = side_by_side([res_ref[n, :, g * 128 : (g + 1) * 128] for n in pick], lane)
                    wide = jnp.concatenate(v, axis=1)
                    for t in range(3):
                        out_ref[o * 4 + g, t, :, group * 384 : group * 384 + 128 * len(v)] = wide[
                            2 * t : 2 * t + 2
                        ].astype(BF16)
            return carry

        lax.fori_loop(0, 32, owner, 0)


def x_lags(order, keep, other, tx, coef):
    block = pl.BlockSpec((OFFS, 5, 8, LAG), lambda i: (i, 0, 0, 0))
    return pl.pallas_call(
        x_lag_kernel,
        grid=(REFS,),
        in_specs=[
            pl.BlockSpec(memory_space=pltpu.SMEM),
            block,
            block,
            pl.BlockSpec((2 * LAG, 512), lambda i: (0, 0)),
            pl.BlockSpec((4, 8, LAG), lambda i: (0, 0, 0)),
        ],
        out_specs=pl.BlockSpec((DEVICES, 3, 2, WIDE), lambda i: (0, 0, 0, 0)),
        out_shape=jax.ShapeDtypeStruct((DEVICES, 3, 2, WIDE), BF16),
        scratch_shapes=[pltpu.VMEM(((PAIRS + 1) * 5, 8, 512), F32)],
        compiler_params=pltpu.CompilerParams(vmem_limit_bytes=VMEM_BYTES),
        name="x_lags",
    )(order, keep, other, tx, coef)


def z_lag_kernel(x_ref, hi_ref, lo_ref, out_ref, full_ref):
    core = pl.program_id(0)

    def gather(i, carry):
        x = x_ref[pl.ds(8 * i, 8)].astype(F32)
        rows = jnp.concatenate([x[c, t] for c in range(8) for t in range(3)], axis=0)
        full_ref[pl.ds(pl.multiple_of(48 * i, 16), 48), :] = rows.astype(BF16)
        return carry

    lax.fori_loop(0, CHIPS // 8, gather, 0)
    dims = (((0,), (0,)), ((), ()))
    for group in range(4):
        count = 4 if group < 3 else 2
        x = full_ref[:, group * 384 : group * 384 + (384 if group < 3 else 256)]
        acc = lax.dot_general(x, hi_ref[...], dims, preferred_element_type=F32)
        acc = acc + lax.dot_general(x, lo_ref[...], dims, preferred_element_type=F32)
        acc = acc * (2.0 / float(NX * NZ) ** 2)
        for n in range(count):
            plane = acc[QB * n : QB * n + QB]
            if group < 3:
                ij = jnp.where(core == 0, n, 8 - n)
                out_ref[group, ij] = plane
            elif n == 0:
                out_ref[core, 4] = plane
            else:

                @pl.when(core == 0)
                def _():
                    out_ref[2, 4] = plane


def z_lags(x, hi, lo):
    return pl.pallas_call(
        z_lag_kernel,
        grid=(2,),
        in_specs=[
            pl.BlockSpec((CHIPS, 3, 2, WIDE), lambda i: (i, 0, 0, 0)),
            pl.BlockSpec((CHIPS * 6, LAG), lambda i: (0, 0)),
            pl.BlockSpec((CHIPS * 6, LAG), lambda i: (0, 0)),
        ],
        out_specs=pl.BlockSpec((SLOTS, 9, QB, LAG), lambda i: (0, 0, 0, 0)),
        out_shape=jax.ShapeDtypeStruct((SLOTS, 9, QB, LAG), F32),
        scratch_shapes=[pltpu.VMEM((CHIPS * 6, WIDE), BF16)],
        compiler_params=pltpu.CompilerParams(vmem_limit_bytes=VMEM_BYTES),
        name="z_lags",
    )(x, hi, lo)


def per_device(velocity, ref_planes, partner_offsets, band_owner):
    core = lax.axis_index("core").astype(jnp.int32)
    first_chip = (lax.axis_index("y") == 0) & (lax.axis_index("x") == 0) & (lax.axis_index("z") == 0)

    forward_z = jnp.asarray(z_table()).astype(BF16)
    parcels = z_transform(forward_z, velocity.reshape(3, LAG, NZ))
    arrived = lax.all_to_all(parcels, ("y", "x", "core", "z"), split_axis=0, concat_axis=0, tiled=True)

    pair = jnp.arange(PAIRS, dtype=jnp.int32)
    same = band_owner[:, None] == band_owner[None, :]
    slot = jnp.sum((same & (pair[None, :] < pair[:, None])).astype(jnp.int32), axis=1)
    dest = ((band_owner % 2) * 16 + band_owner // 2) * SLOTS + slot
    hit = dest[None, :] == jnp.arange(32 * SLOTS, dtype=jnp.int32)[:, None]
    table = PAIRS + jnp.sum(jnp.where(hit, pair[None, :] - PAIRS, 0), axis=1)
    order = jnp.concatenate([table, core[None]])

    row = jnp.arange(8, dtype=jnp.int32)
    sign = jnp.where(core == 0, 1.0, -1.0)
    extra = row % 4 == 3
    halved = first_chip & (core == 0) & ((row == 0) | (row == 3))
    scale = jnp.broadcast_to(jnp.where(halved, math.sqrt(0.5), 1.0)[:, None], (8, LAG)).astype(F32)
    coef = jnp.stack(
        [
            jnp.where(extra, sign, 1.0),
            jnp.where(extra, -sign, 1.0),
            jnp.where(first_chip & (row == 4), 1.0, 0.0),
            jnp.where(row < 4, 1.0, -1.0),
        ]
    )
    coef = jnp.broadcast_to(coef[:, :, None], (4, 8, LAG)).astype(F32)

    send, keep = products(
        jnp.concatenate([ref_planes, partner_offsets, core[None]]),
        arrived,
        jnp.asarray(x_table()).astype(BF16),
        scale,
    )
    other = lax.ppermute(send, "core", [(0, 1), (1, 0)])
    spread = x_lags(order, keep, other, jnp.asarray(x_lag_table()).astype(BF16), coef)
    landed = lax.all_to_all(spread, ("core", "y", "x", "z"), split_axis=0, concat_axis=0, tiled=True)
    full = jnp.asarray(z_lag_table())
    hi = full.astype(BF16)
    lo = (full - hi.astype(F32)).astype(BF16)
    return z_lags(landed, hi, lo)


def solution(mesh):
    inner = Mesh(mesh.devices.reshape(4, 4, 2, 4), ("y", "x", "core", "z"))
    gy = ("y", "x", "core")
    return jax.shard_map(
        per_device,
        mesh=inner,
        in_specs=(P(None, gy, "z", None), P(), P(), P()),
        out_specs=P(gy, None, "z", None),
        check_vma=False,
    )
```

time: 165 us -> 162 us (0.982)
  blocking collectives: 41.1 us -> 33.8 us
  waiting for transfers between devices: 44.3 us -> 50.1 us
  Pallas kernels: 55.5 us -> 61.1 us
  other arithmetic: 5.17 us -> 1.56 us
  local copies, waits for them, and re-layouts: 6.12 us -> 3.42 us
    all_to_all x1, blocking collectives: 41.1 us -> 33.8 us  [per_device(): lax.all_to_all(spread, ('core', 'y', 'x', 'z'), split_axis=0, concat_axis...]
    all_to_all x1, waiting for transfers between devices: 39 us -> 45.5 us  [per_device(): lax.all_to_all(parcels, ('y', 'x', 'core', 'z'), split_axis=0, concat_axi...]
    pallas_call x3 -> x4, Pallas kernels: 55.5 us -> 61.1 us  [the longest x1 31.1 us: products(): pl.pallas_call(product_kernel, in_specs=[smem, vmem, vmem, vmem], out_spe...]
    convert_element_type x1 -> x0, other arithmetic: 2.41 us -> none  [per_device(): (keep.astype(F32) + other.astype(F32)).astype(BF16).reshape(CHIPS, 8, 2688)]
    slice x3 -> x0, local copies, waits for them, and re-layouts: 2.17 us -> none  [the longest x2 1.39 us: per_device(): table[:, 1]]
  transfers between devices with their start and end apart: 2 -> 2, of which waited for: 2 -> 2; matrix products, arithmetic and copies ran while one was open for 4% -> 1% of each run, Pallas kernels for 0% -> 0%
where the time goes in v2:
time: 162 us
  Pallas kernels  61.1 us (38%)
  waiting for transfers between devices  50.1 us (31%)
  blocking collectives  33.8 us (21%)
  starting transfers between devices  11.5 us (7%)
  local copies, waits for them, and re-layouts  3.42 us (2%)
    all_to_all x1, waiting for transfers between devices, per_device(): lax.all_to_all(parcels, ('y', 'x', 'core', 'z'), split_axis=0, concat_axi...  45.5 us
    all_to_all x1, blocking collectives, per_device(): lax.all_to_all(spread, ('core', 'y', 'x', 'z'), split_axis=0, concat_axis...  33.8 us
    pallas_call x1, Pallas kernels, products(): pl.pallas_call(product_kernel, in_specs=[smem, vmem, vmem, vmem], out_spe...  31.1 us
    pallas_call x1, Pallas kernels, z_transform(): pl.pallas_call(z_kernel, grid=(3,), in_specs=[pl.BlockSpec((NZ, NZ), lamb...  11.6 us
    all_to_all x1, starting transfers between devices, per_device(): lax.all_to_all(parcels, ('y', 'x', 'core', 'z'), split_axis=0, concat_axi...  11.5 us
    pallas_call x1, Pallas kernels, x_lags(): pl.pallas_call(x_lag_kernel, grid=(REFS,), in_specs=[pl.BlockSpec(memory_...  10.5 us
    pallas_call x1, Pallas kernels, z_lags(): pl.pallas_call(z_lag_kernel, grid=(2,), in_specs=[pl.BlockSpec((CHIPS, 3,...  7.86 us
    ppermute x1, waiting for transfers between devices, per_device(): other = lax.ppermute(send, 'core', [(0, 1), (1, 0)])  4.62 us
  transfers between devices with their start and end apart: 2, of which 2 were waited for; matrix products, arithmetic and copies ran while one was open for 1% of the time, Pallas kernels for 0%

profile of v2, /device:TPU:1, one launch (start us, length us, event | category | flops | bytes accessed | tf_op | source)
XLA Modules:
  0.0 161.6 jit_solution(13090945798654018194)
XLA Ops:
  0.0 11.6 %z_transform.1 = bf16[128,3,3,4,384]{4,3,2,1,0:T(4,128)(2,1)} custom-call(bf16[1536,1536]{1,0:T(8,128)(2,1)} %constant.90.table_ref, bf16[3,384,1536]{2,1,0:T(8,128)(2,1)} %bitcast.2), custom_call_target="tpu_custom_call" | custom-call | tf_op jit(solution)/shard_map/z_transform/pallas_call | solution.py:113
  11.6 0.0 copy-start.2
  11.6 0.0 copy-start.3
  11.6 11.5 %all-to-all-start = ((bf16[128,3,3,4,384]{4,3,2,1,0:T(4,128)(2,1)}), bf16[128,3,3,4,384]{4,3,2,1,0:T(4,128)(2,1)S(1)}, u32[]{:S(2)}, u32[]{:S(2)}) async-start(bf16[128,3,3,4,384]{4,3,2,1,0:T(4,128)(2,1)} %z_transform.1), calls=%async_computation | async-start | bytes 7077888 | tf_op jit(solution)/shard_map/all_to_all | solution.py:371
  23.1 0.0 copy-done.2
  23.1 0.0 copy-done.3
  23.1 0.6 pad_add_fusion.1.planes_ref
  23.7 45.5 %all-to-all-done.arr_ref = bf16[128,3,3,4,384]{4,3,2,1,0:T(4,128)(2,1)S(1)} async-done(((bf16[128,3,3,4,384]{4,3,2,1,0:T(4,128)(2,1)}), bf16[128,3,3,4,384]{4,3,2,1,0:T(4,128)(2,1)S(1)}, u32[]{:S(2)}, u32[]{:S(2)}) %all-to-all-start) | async-done | bytes 3538976 | tf_op jit(solution)/shard_map/all_to_all | solution.py:371
  69.2 0.0 copy-start
  69.2 0.7 broadcast_in_dim.68.coef_ref
  70.0 1.1 copy-done
  71.0 0.0 copy-start.4
  71.0 31.1 %products.1 = (f32[48,5,8,384]{3,2,1,0:T(8,128)}, f32[48,5,8,384]{3,2,1,0:T(8,128)}) custom-call(s32[15]{0:T(128)} %pad_add_fusion.1.planes_ref, bf16[128,3,3,4,384]{4,3,2,1,0:T(4,128)(2,1)} %copy-done, bf16[4,4,768,256]{3,2,1,0:T(8,128)(2,1)} %constant.91.wx_ref, f32[8,384]{1,0:T(8,128)} %broadcast_in_dim.68.coef_ref), custom_call_target="tpu_custom_call" | custom-call | tf_op jit(solution)/shard_map/products/pallas_call | solution.py:238
  102.2 0.0 collective-permute-start
  102.2 0.0 copy-done.4
  102.2 0.2 convert_reduce_fusion
  102.4 0.1 select_reduce_fusion
  102.5 0.6 pad_add_fusion.order_ref
  103.1 4.6 %collective-permute-done.other_ref = f32[48,5,8,384]{3,2,1,0:T(8,128)S(1)} collective-permute-done((f32[48,5,8,384]{3,2,1,0:T(8,128)}, f32[48,5,8,384]{3,2,1,0:T(8,128)S(1)}, u32[]{:S(2)}, u32[]{:S(2)}) %collective-permute-start) | collective-permute-done | bytes 2949152 | tf_op jit(solution)/shard_map/ppermute | solution.py:402
  107.8 0.0 copy-start.1
  107.8 0.8 broadcast_in_dim.74.coef_ref
  108.5 0.8 copy-done.1
  109.4 10.5 %x_lags.1 = bf16[128,3,2,1408]{3,2,1,0:T(2,128)(2,1)} custom-call(s32[97]{0:T(128)} %pad_add_fusion.order_ref, f32[48,5,8,384]{3,2,1,0:T(8,128)} %get-tuple-element.7.keep_ref, f32[48,5,8,384]{3,2,1,0:T(8,128)} %copy-done.1, bf16[768,512]{1,0:T(8,128)(2,1)} %constant.92.tx_ref, f32[4,8,384]{2,1,0:T(8,128)} %broadcast_in_dim.74.coef_ref), custom_call_target="tpu_custom_call" | custom-call | tf_op jit(solution)/shard_map/x_lags/pallas_call | solution.py:299
  119.9 33.8 %all_to_all.10.x_ref = bf16[128,3,2,1408]{3,2,1,0:T(2,128)(2,1)} all-to-all(bf16[128,3,2,1408]{3,2,1,0:T(2,128)(2,1)} %x_lags.1), channel_id=1, replica_groups=mesh['y'=4,'x'=4,'core'=2,'z'=4] {'core','y','x','z'}, dimensions={0} | all-to-all | bytes 4325376 | tf_op jit(solution)/shard_map/all_to_all | solution.py:404
  153.7 7.9 %z_lags.1 = f32[3,9,96,384]{3,2,1,0:T(8,128)} custom-call(bf16[128,3,2,1408]{3,2,1,0:T(2,128)(2,1)} %all_to_all.10.x_ref, bf16[384,384]{1,0:T(8,128)(2,1)} %constant.93.hi_ref, bf16[384,384]{1,0:T(8,128)(2,1)} %constant.96.lo_ref), custom_call_target="tpu_custom_call" | custom-call | tf_op jit(solution)/shard_map/z_lags/pallas_call | solution.py:349
  (6 shorter events, 0.1 us)
Async XLA Ops:
  11.6 11.5 %copy-start.2 = (s32[8]{0:T(128)S(1)}, s32[8]{0:T(128)}, u32[]{:S(2)}) copy-start(s32[8]{0:T(128)} %param.10) | copy-start | bytes 100
  11.6 11.5 %copy-start.3 = (s32[6]{0:T(128)S(1)}, s32[6]{0:T(128)}, u32[]{:S(2)}) copy-start(s32[6]{0:T(128)} %param.9) | copy-start | bytes 76
  11.6 57.6 %all-to-all-start = ((bf16[128,3,3,4,384]{4,3,2,1,0:T(4,128)(2,1)}), bf16[128,3,3,4,384]{4,3,2,1,0:T(4,128)(2,1)S(1)}, u32[]{:S(2)}, u32[]{:S(2)}) async-start(bf16[128,3,3,4,384]{4,3,2,1,0:T(4,128)(2,1)} %z_transform.1), calls=%async_computation | async-start | bytes 7077888 | tf_op jit(solution)/shard_map/all_to_all | solution.py:371
  69.2 1.8 %copy-start = (bf16[128,3,3,4,384]{4,3,2,1,0:T(4,128)(2,1)}, bf16[128,3,3,4,384]{4,3,2,1,0:T(4,128)(2,1)S(1)}, u32[]{:S(2)}) copy-start(bf16[128,3,3,4,384]{4,3,2,1,0:T(4,128)(2,1)S(1)} %all-to-all-done.arr_ref) | copy-start | bytes 10616836
  71.0 31.2 %copy-start.4 = (s32[48]{0:T(128)S(1)}, s32[48]{0:T(128)}, u32[]{:S(2)}) copy-start(s32[48]{0:T(128)} %param.11) | copy-start | bytes 580
  102.2 5.6 %collective-permute-start = (f32[48,5,8,384]{3,2,1,0:T(8,128)}, f32[48,5,8,384]{3,2,1,0:T(8,128)S(1)}, u32[]{:S(2)}, u32[]{:S(2)}) collective-permute-start(f32[48,5,8,384]{3,2,1,0:T(8,128)} %get-tuple-element.8), channel_id=1, source_target_pairs={{0,4},{4,0},{1,5},{5,1},{2,6},{6,2},{3,7},{7,3},{8,12},{12,8},{9,1... | collective-permute-start | bytes 8847368 | tf_op jit(solution)/shard_map/ppermute | solution.py:402
  107.8 1.6 copy-start.1

commit v3 on v2

v3 whole, which is shorter than its diff:
```python
import math

import jax
import jax.numpy as jnp
import numpy as np
from jax import lax
from jax.experimental import pallas as pl
from jax.experimental.pallas import tpu as pltpu
from jax.sharding import Mesh, PartitionSpec as P

NX = 1536
NZ = 1536
LAG = 384
NY = 32
REFS = 6
OFFS = 8
PAIRS = REFS * OFFS
SLOTS = 3
CHIPS = 64
DEVICES = 128
QB = 96
F32 = jnp.float32
BF16 = jnp.bfloat16
WIDE = 1408
STEP = 8
MIB = 1024 * 1024


def fold_of(chip, k):
    quarter = CHIPS // 4
    if chip < 2 * quarter:
        return 12 * (chip % quarter) + 4 * k + 2 * (chip // quarter)
    return 6 * (chip - 2 * quarter) + 2 * k + 1


def modes_of(chip, core):
    out = []
    for k in range(3):
        j = fold_of(chip, k)
        if core == 0:
            out.append(j)
        else:
            out.append(LAG // 2 if j == 0 else LAG - j)
    return out


def z_table():
    z = np.arange(NZ // 2)
    order = [(0, 0), (0, 1), (0, 2), (1, 3), (0, 3), (0, 4), (0, 5), (1, 4), (1, 0), (1, 1), (1, 2), (1, 5)]
    rows = []
    for gy in range(32):
        for gx in range(4):
            core = gy % 2
            kzs = modes_of((gy // 2) * 4 + gx, core)
            six = kzs + [k + LAG for k in kzs]
            sign = 1.0 if core == 0 else -1.0
            for part, pos in order:
                angle = 2.0 * math.pi / NZ * ((six[pos] * z) % NZ)
                rows.append(np.cos(angle) if part == 0 else -sign * np.sin(angle))
    return np.stack(rows).astype(np.float32)


def x_table():
    out = np.zeros((4, 2, LAG, 2, 4, 128), np.float64)
    x = np.arange(LAG)[:, None]
    lane = np.arange(QB)[None, :]
    for r in range(4):
        for m in range(4):
            angle = 2.0 * math.pi / NX * ((x * (4 * (lane + QB * m) + r)) % NX)
            out[r, 0, :, 0, m, :QB] = np.cos(angle)
            out[r, 1, :, 0, m, :QB] = np.sin(angle)
            out[r, 0, :, 1, m, :QB] = -np.sin(angle)
            out[r, 1, :, 1, m, :QB] = np.cos(angle)
    return out.reshape(4, 2 * LAG, 4, 256).transpose(2, 0, 1, 3).astype(np.float32)


def x_lag_table():
    out = np.zeros((2, 4, QB, 4, 128), np.float64)
    q = np.arange(QB)[:, None]
    col = np.arange(QB)[None, :]
    for r in range(4):
        for g in range(4):
            angle = 2.0 * math.pi / LAG * (((4 * q + r) * (QB * g + col)) % LAG)
            out[0, r, :, g, :QB] = np.cos(angle)
            out[1, r, :, g, :QB] = -np.sin(angle)
    return out.reshape(2 * LAG, 512).astype(np.float32)


def z_lag_table():
    out = np.zeros((CHIPS, 6, LAG), np.float64)
    t = np.arange(LAG)
    for chip in range(CHIPS):
        for k in range(3):
            j = fold_of(chip, k)
            if j == 0:
                out[chip, k] = (1.0 + (-1.0) ** t) / 2.0
                out[chip, 3 + k] = (1.0 - (-1.0) ** t) / 2.0
            else:
                angle = 2.0 * math.pi / LAG * ((j * t) % LAG)
                out[chip, k] = np.cos(angle)
                out[chip, 3 + k] = -np.sin(angle)
    return out.reshape(CHIPS * 6, LAG).astype(np.float32)


def z_kernel(table_ref, vel_ref, out_ref, sum_ref, twist_ref, odd_ref):
    step = pl.program_id(0)
    quarter = NZ // 4
    first = lax.broadcasted_iota(jnp.int32, (4, LAG), 0) == 0

    def part(n):
        return vel_ref[:, :, n * quarter : (n + 1) * quarter].reshape(3 * LAG, quarter)

    def emit(field_ref, special):
        acc = lax.dot_general(
            table_ref[:, : field_ref.shape[1]],
            field_ref[...],
            (((1,), (1,)), ((), ())),
            preferred_element_type=F32,
        )
        for d in range(DEVICES // 4):
            for t in range(3):
                row = 12 * d + 4 * t
                for c in range(3):
                    piece = acc[row : row + 4, c * LAG : (c + 1) * LAG]
                    if special and d == 0 and t != 1:
                        piece = jnp.where(first, piece * math.sqrt(0.5), piece)
                    out_ref[d, c, t] = piece.astype(BF16)

    @pl.when(step == 0)
    def _():
        for c in range(3):
            q = [vel_ref[c, :, n * quarter : (n + 1) * quarter].astype(F32) for n in range(4)]
            even, other = q[0] + q[2], q[1] + q[3]
            sum_ref[c * LAG : (c + 1) * LAG] = (even + other).astype(BF16)
            twist_ref[c * LAG : (c + 1) * LAG] = (even - other).astype(BF16)
        emit(sum_ref, True)

    @pl.when(step == 1)
    def _():
        emit(twist_ref, False)

    @pl.when(step == 2)
    def _():
        odd_ref[:, :quarter] = part(0) - part(2)
        odd_ref[:, quarter:] = part(1) - part(3)

    @pl.when(step >= 2)
    def _():
        emit(odd_ref, False)


def z_transform(table, vel):
    return pl.pallas_call(
        z_kernel,
        grid=(4,),
        in_specs=[
            pl.BlockSpec((NZ // 4, NZ // 2), lambda i: (i, 0)),
            pl.BlockSpec((3, LAG, NZ), lambda i: (0, 0, 0)),
        ],
        out_specs=pl.BlockSpec((DEVICES // 4, 3, 3, 4, LAG), lambda i: (i, 0, 0, 0, 0)),
        out_shape=jax.ShapeDtypeStruct((DEVICES, 3, 3, 4, LAG), BF16),
        scratch_shapes=[
            pltpu.VMEM((3 * LAG, NZ // 4), BF16),
            pltpu.VMEM((3 * LAG, NZ // 4), BF16),
            pltpu.VMEM((3 * LAG, NZ // 2), BF16),
        ],
        compiler_params=pltpu.CompilerParams(vmem_limit_bytes=60 * MIB),
        name="z_transform",
    )(table, vel)


def side_by_side(pieces, lane):
    rolled = [pltpu.roll(v, 96 * n % 128, 1) if n else v for n, v in enumerate(pieces)]
    out = [jnp.where(lane < 96, rolled[0], rolled[1])]
    if len(pieces) == 2:
        return out + [jnp.where(lane < 64, rolled[1], 0.0)]
    out.append(jnp.where(lane < 64, rolled[1], rolled[2]))
    out.append(jnp.where(lane < 32, rolled[2], rolled[3]))
    return out


def pair_loop(planes_ref, u_ref, out_ref, kept):
    low = lax.broadcasted_iota(jnp.int32, (8, 128), 0) < 4
    chosen = range(5) if kept else range(8, 3, -1)

    def pair_products(p, carry):
        plane = planes_ref[p // OFFS]
        first = plane * 3
        second = (plane + planes_ref[REFS + p % OFFS]) * 3
        for lg in range(3):
            at = slice(lg * 128, (lg + 1) * 128)
            sums = {}
            for m in range(4):
                left, right = {}, {}
                for i in sorted({ij // 3 for ij in chosen}):
                    re, im = u_ref[m, first + i, :, at], u_ref[4 + m, first + i, :, at]
                    left[i] = (re, im, re - im)
                for j in range(3):
                    re, im = u_ref[m, second + j, :, at], u_ref[4 + m, second + j, :, at]
                    right[j] = (re, im, re + im)
                for ij in chosen:
                    terms = [a * b for a, b in zip(left[ij // 3], right[ij % 3])]
                    sums[ij] = terms if m == 0 else [s + t for s, t in zip(sums[ij], terms)]
            for n, ij in enumerate(chosen):
                rr, ii, mixed = sums[ij]
                re = rr + ii
                im = mixed + (ii - rr)
                out_ref[p, n, :, at] = jnp.where(low, re, im) + pltpu.roll(jnp.where(low, im, re), 4, 0)
        return carry

    lax.fori_loop(0, PAIRS, pair_products, 0)


def keep_kernel(planes_ref, u_ref, keep_ref):
    pair_loop(planes_ref, u_ref, keep_ref, True)


def send_kernel(planes_ref, arr_ref, wx_hbm, send_ref, u_ref, wx_ref, sem, lhs_ref, tmp0_ref, tmp1_ref):
    fetch = pltpu.make_async_copy(wx_hbm, wx_ref, sem)
    fetch.start()
    core = planes_ref[REFS + OFFS]

    def butterfly(i, carry):
        pieces = [[] for _ in range(4)]
        for yy in range(2):
            for c in range(3):
                comp = jnp.where(core == 0, c, 2 - c)
                re, im = [], []
                for g in range(4):
                    src = (2 * i + yy) * 4 + g
                    t0 = arr_ref[src, comp, 0].astype(F32)
                    t1 = arr_ref[src, comp, 1].astype(F32)
                    t2 = arr_ref[src, comp, 2].astype(F32)
                    re.append(jnp.concatenate([t0, t1], axis=0))
                    im.append(jnp.concatenate([t2, t0[3:4], t1[3:4], t2[3:4], t2[3:4]], axis=0))
                s02r, d02r = re[0] + re[2], re[0] - re[2]
                s02i, d02i = im[0] + im[2], im[0] - im[2]
                s13r, d13r = re[1] + re[3], re[1] - re[3]
                s13i, d13i = im[1] + im[3], im[1] - im[3]
                parts = [
                    (s02r + s13r, s02i + s13i),
                    (d02r + d13i, d02i - d13r),
                    (s02r - s13r, s02i - s13i),
                    (d02r - d13i, d02i + d13r),
                ]
                for r in range(4):
                    pieces[r].append(parts[r])
        for r in range(4):
            for h in range(3):
                lo, hi = pieces[r][2 * h], pieces[r][2 * h + 1]
                row = pl.multiple_of(i * 48 + 16 * h, 16)
                for part in range(2):
                    both = jnp.concatenate([lo[part], hi[part]], axis=0).astype(BF16)
                    lhs_ref[r, pl.ds(row, 16), part * LAG : (part + 1) * LAG] = both
        return carry

    lax.fori_loop(0, NY // 2, butterfly, 0)

    lane = lax.broadcasted_iota(jnp.int32, (8, 128), 1)

    fetch.wait()
    tmp = (tmp0_ref, tmp1_ref)
    for tile in range(5):
        for r in range(4):
            if tile < 4:
                out = jnp.dot(lhs_ref[r], wx_ref[tile, r], preferred_element_type=F32)
                tmp[tile % 2][r] = out.reshape(3 * NY, 8, 256)
            if tile > 0:
                done = tmp[(tile - 1) % 2]
                for row in range(24 * r, 24 * r + 24):
                    for h in range(2):
                        v = side_by_side([done[q, row, :, h * 128 : (h + 1) * 128] for q in range(4)], lane)
                        u_ref[2 * tile - 2 + h, row] = jnp.concatenate(v, axis=1)

    pair_loop(planes_ref, u_ref, send_ref, False)


def send_products(planes, arr, wx):
    vmem = pl.BlockSpec(memory_space=pltpu.VMEM)
    return pl.pallas_call(
        send_kernel,
        in_specs=[pl.BlockSpec(memory_space=pltpu.SMEM), vmem, pl.BlockSpec(memory_space=pltpu.HBM)],
        out_specs=[vmem, vmem],
        out_shape=[
            jax.ShapeDtypeStruct((PAIRS, 5, 8, LAG), F32),
            jax.ShapeDtypeStruct((8, 3 * NY, 8, LAG), F32),
        ],
        scratch_shapes=[
            pltpu.VMEM((4, 4, 2 * LAG, 256), BF16),
            pltpu.SemaphoreType.DMA,
            pltpu.VMEM((4, 24 * NY, 2 * LAG), BF16),
            pltpu.VMEM((4, 3 * NY, 8, 256), F32),
            pltpu.VMEM((4, 3 * NY, 8, 256), F32),
        ],
        compiler_params=pltpu.CompilerParams(vmem_limit_bytes=28 * MIB),
        name="send_products",
    )(planes, arr, wx)


def keep_products(planes, u):
    vmem = pl.BlockSpec(memory_space=pltpu.VMEM)
    return pl.pallas_call(
        keep_kernel,
        in_specs=[pl.BlockSpec(memory_space=pltpu.SMEM), vmem],
        out_specs=vmem,
        out_shape=jax.ShapeDtypeStruct((PAIRS, 5, 8, LAG), F32),
        cost_estimate=pl.CostEstimate(flops=60_000_000, bytes_accessed=12_000_000, transcendentals=0),
        compiler_params=pltpu.CompilerParams(vmem_limit_bytes=8 * MIB),
        name="keep_products",
    )(planes, u)


def x_lag_kernel(order_ref, keep_ref, other_ref, tx_ref, coef_ref, out_ref, res_ref):
    rows = STEP * 5
    swap = coef_ref[0] > 0.5
    sign = coef_ref[1]
    mirror = coef_ref[2]
    low = lax.broadcasted_iota(jnp.int32, (8, 512), 0) < 3

    def group(i, carry):
        halves = [[], []]
        for n in range(rows):
            mine = keep_ref[i * STEP + n // 5, n % 5]
            theirs = other_ref[i * STEP + n // 5, n % 5]
            total = mine + theirs
            apart = (mine - theirs) * mirror
            halves[0].append(jnp.where(swap, pltpu.roll(apart, 4, 0), total))
            halves[1].append(jnp.where(swap, apart, pltpu.roll(total, 4, 0) * sign))
        lhs = jnp.concatenate([jnp.concatenate(h, axis=0) for h in halves], axis=1)
        high = lhs.astype(BF16)
        rest = (lhs - high.astype(F32)).astype(BF16)
        out = jnp.dot(high, tx_ref[...], preferred_element_type=F32)
        out = out + jnp.dot(rest, tx_ref[...], preferred_element_type=F32)
        for n in range(rows):
            x = out[8 * n : 8 * n + 8]
            res_ref[i * rows + n] = jnp.where(low, x, pltpu.roll(x, 7, 0))
        return carry

    lax.fori_loop(0, PAIRS // STEP, group, 0)
    res_ref[PAIRS * 5 : PAIRS * 5 + 5] = jnp.zeros((5, 8, 512), F32)
    core = order_ref[32 * SLOTS]
    lane = lax.broadcasted_iota(jnp.int32, (8, 128), 1)

    def owner(o, carry):
        at = [order_ref[o * SLOTS + s] * 5 for s in range(SLOTS)]
        index = [at[f // 4] + f % 4 for f in range(12)]
        index.append(jnp.where(core == 0, at[0], at[1]) + 4)
        index.append(jnp.where(core == 0, at[2] + 4, PAIRS * 5))
        for g in range(4):
            for group in range(4):
                pick = index[4 * group : 4 * group + 4]
                v = side_by_side([res_ref[n, :, g * 128 : (g + 1) * 128] for n in pick], lane)
                wide = jnp.concatenate(v, axis=1)
                for t in range(3):
                    out_ref[o * 4 + g, t, :, group * 384 : group * 384 + 128 * len(v)] = wide[
                        2 * t : 2 * t + 2
                    ].astype(BF16)
        return carry

    lax.fori_loop(0, 32, owner, 0, unroll=2)


def x_lags(order, keep, other, tx, coef):
    vmem = pl.BlockSpec(memory_space=pltpu.VMEM)
    return pl.pallas_call(
        x_lag_kernel,
        in_specs=[pl.BlockSpec(memory_space=pltpu.SMEM), vmem, vmem, vmem, vmem],
        out_specs=vmem,
        out_shape=jax.ShapeDtypeStruct((DEVICES, 3, 2, WIDE), BF16),
        scratch_shapes=[pltpu.VMEM(((PAIRS + 1) * 5, 8, 512), F32)],
        compiler_params=pltpu.CompilerParams(vmem_limit_bytes=20 * MIB),
        name="x_lags",
    )(order, keep, other, tx, coef)


def z_lag_kernel(x_ref, table_ref, out_hbm, full_ref, plane_ref, sem):
    def gather(i, carry):
        x = x_ref[pl.ds(8 * i, 8)].astype(F32)
        rows = jnp.concatenate([x[c, t] for c in range(8) for t in range(3)], axis=0)
        full_ref[pl.ds(pl.multiple_of(48 * i, 16), 48), :] = rows.astype(BF16)
        return carry

    lax.fori_loop(0, 2 * CHIPS // 8, gather, 0)
    dims = (((0,), (0,)), ((), ()))
    half = CHIPS * 6

    def planes(core, group):
        stop = group * 384 + (384 if group < 3 else 256)
        x = full_ref[core * half : (core + 1) * half, group * 384 : stop]
        acc = lax.dot_general(x, table_ref[...], dims, preferred_element_type=F32)
        return acc * (2.0 / float(NX * NZ) ** 2)

    extra = planes(0, 3)
    plane_ref[0, 4] = extra[:QB]
    plane_ref[2, 4] = extra[QB : 2 * QB]
    plane_ref[1, 4] = planes(1, 3)[:QB]
    copies = []
    for slot in range(SLOTS):
        for core in range(2):
            acc = planes(core, slot)
            for n in range(4):
                plane_ref[slot, n if core == 0 else 8 - n] = acc[QB * n : QB * n + QB]
        copies.append(pltpu.make_async_copy(plane_ref.at[slot], out_hbm.at[slot], sem.at[slot]))
        copies[-1].start()
    for copy in copies:
        copy.wait()


def z_lags(x, table):
    vmem = pl.BlockSpec(memory_space=pltpu.VMEM)
    return pl.pallas_call(
        z_lag_kernel,
        in_specs=[vmem, vmem],
        out_specs=pl.BlockSpec(memory_space=pltpu.HBM),
        out_shape=jax.ShapeDtypeStruct((SLOTS, 9, QB, LAG), F32),
        scratch_shapes=[
            pltpu.VMEM((2 * CHIPS * 6, WIDE), BF16),
            pltpu.VMEM((SLOTS, 9, QB, LAG), F32),
            pltpu.SemaphoreType.DMA((SLOTS,)),
        ],
        compiler_params=pltpu.CompilerParams(vmem_limit_bytes=20 * MIB),
        name="z_lags",
    )(x, table)


def per_device(velocity, ref_planes, partner_offsets, band_owner):
    core = lax.axis_index("core").astype(jnp.int32)
    first_chip = (lax.axis_index("y") == 0) & (lax.axis_index("x") == 0) & (lax.axis_index("z") == 0)

    forward_z = jnp.asarray(z_table()).astype(BF16)
    parcels = z_transform(forward_z, velocity.reshape(3, LAG, NZ))
    arrived = lax.all_to_all(parcels, ("y", "x", "core", "z"), split_axis=0, concat_axis=0, tiled=True)

    pair = jnp.arange(PAIRS, dtype=jnp.int32)
    same = band_owner[:, None] == band_owner[None, :]
    slot = jnp.sum((same & (pair[None, :] < pair[:, None])).astype(jnp.int32), axis=1)
    dest = ((band_owner % 2) * 16 + band_owner // 2) * SLOTS + slot
    hit = dest[None, :] == jnp.arange(32 * SLOTS, dtype=jnp.int32)[:, None]
    table = PAIRS + jnp.sum(jnp.where(hit, pair[None, :] - PAIRS, 0), axis=1)
    order = jnp.concatenate([table, core[None]])

    row = jnp.arange(8, dtype=jnp.int32)
    coef = jnp.stack(
        [
            jnp.where(first_chip & (row == 4), 1.0, 0.0),
            jnp.where(row < 4, 1.0, -1.0),
            jnp.broadcast_to(jnp.where(core == 0, 1.0, -1.0), (8,)),
        ]
    )
    coef = jnp.broadcast_to(coef[:, :, None], (3, 8, LAG)).astype(F32)
    planes = jnp.concatenate([ref_planes, partner_offsets, core[None]])
    planes, order, coef, arrived = lax.optimization_barrier((planes, order, coef, arrived))

    forward_x = pltpu.with_memory_space_constraint(jnp.asarray(x_table()).astype(BF16), pltpu.HBM)
    send, spectra = send_products(planes, arrived, forward_x)
    other = lax.ppermute(send, "core", [(0, 1), (1, 0)])
    keep = keep_products(planes, spectra)
    spread = x_lags(order, keep, other, jnp.asarray(x_lag_table()).astype(BF16), coef)
    landed = lax.all_to_all(spread, ("core", "y", "x", "z"), split_axis=0, concat_axis=0, tiled=True)
    return z_lags(landed, jnp.asarray(z_lag_table()).astype(BF16))


def solution(mesh):
    inner = Mesh(mesh.devices.reshape(4, 4, 2, 4), ("y", "x", "core", "z"))
    gy = ("y", "x", "core")
    return jax.shard_map(
        per_device,
        mesh=inner,
        in_specs=(P(None, gy, "z", None), P(), P(), P()),
        out_specs=P(gy, None, "z", None),
        check_vma=False,
    )
```

time: 162 us -> 128 us (0.79)
  Pallas kernels: 61.1 us -> 36 us
  waiting for transfers between devices: 50.1 us -> 46.3 us
  local copies, waits for them, and re-layouts: 3.42 us -> 0.17 us
    pallas_call x4 -> x5, Pallas kernels: 61.1 us -> 36 us  [the longest x1 12.8 us: send_products(): pl.pallas_call(send_kernel, in_specs=[pl.BlockSpec(memory_space=pltpu.SME...]
    ppermute x1, waiting for transfers between devices: 4.62 us -> 0.82 us  [per_device(): other = lax.ppermute(send, 'core', [(0, 1), (1, 0)])]
    unnamed x10, local copies, waits for them, and re-layouts: 1.9 us -> 0.02 us
  transfers between devices with their start and end apart: 2 -> 2, of which waited for: 2 -> 2; matrix products, arithmetic and copies ran while one was open for 1% -> 0% of each run, Pallas kernels for 0% -> 4%
where the time goes in v3:
time: 128 us
  waiting for transfers between devices  46.3 us (36%)
  Pallas kernels  36 us (28%)
  blocking collectives  33.4 us (26%)
  starting transfers between devices  11.6 us (9%)
    all_to_all x1, waiting for transfers between devices, per_device(): lax.all_to_all(parcels, ('y', 'x', 'core', 'z'), split_axis=0, concat_axi...  45.5 us
    all_to_all x1, blocking collectives, per_device(): lax.all_to_all(spread, ('core', 'y', 'x', 'z'), split_axis=0, concat_axis...  33.4 us
    pallas_call x1, Pallas kernels, send_products(): pl.pallas_call(send_kernel, in_specs=[pl.BlockSpec(memory_space=pltpu.SME...  12.8 us
    all_to_all x1, starting transfers between devices, per_device(): lax.all_to_all(parcels, ('y', 'x', 'core', 'z'), split_axis=0, concat_axi...  11.5 us
    pallas_call x1, Pallas kernels, z_transform(): pl.pallas_call(z_kernel, grid=(4,), in_specs=[pl.BlockSpec((NZ // 4, NZ /...  7.65 us
    pallas_call x1, Pallas kernels, x_lags(): pl.pallas_call(x_lag_kernel, in_specs=[pl.BlockSpec(memory_space=pltpu.SM...  6.82 us
    pallas_call x1, Pallas kernels, keep_products(): pl.pallas_call(keep_kernel, in_specs=[pl.BlockSpec(memory_space=pltpu.SME...  4.52 us
    pallas_call x1, Pallas kernels, z_lags(): pl.pallas_call(z_lag_kernel, in_specs=[vmem, vmem], out_specs=pl.BlockSpe...  4.22 us
  transfers between devices with their start and end apart: 2, of which 2 were waited for; matrix products, arithmetic and copies ran while one was open for 0% of the time, Pallas kernels for 4%

profile of v3, /device:TPU:1, one launch (start us, length us, event | category | flops | bytes accessed | tf_op | source)
XLA Modules:
  0.0 128.0 jit_solution(6389800244087604533)
XLA Ops:
  0.0 7.7 %z_transform.1 = bf16[128,3,3,4,384]{4,3,2,1,0:T(4,128)(2,1)} custom-call(bf16[1536,768]{1,0:T(8,128)(2,1)} %constant.73.table_ref, bf16[3,384,1536]{2,1,0:T(8,128)(2,1)} %bitcast.3), custom_call_target="tpu_custom_call" | custom-call | tf_op jit(solution)/shard_map/z_transform/pallas_call | solution.py:153
  7.7 0.0 copy-start.2
  7.7 0.0 copy-start.3
  7.7 0.0 copy-start.4
  7.7 11.5 %all-to-all-start = ((bf16[128,3,3,4,384]{4,3,2,1,0:T(4,128)(2,1)}), bf16[128,3,3,4,384]{4,3,2,1,0:T(4,128)(2,1)S(1)}, u32[]{:S(2)}, u32[]{:S(2)}) async-start(bf16[128,3,3,4,384]{4,3,2,1,0:T(4,128)(2,1)} %z_transform.1), calls=%async_computation | async-start | bytes 7077888 | tf_op jit(solution)/shard_map/all_to_all | solution.py:432
  19.2 0.1 pad.2.clone
  19.3 0.0 copy-done.2
  19.3 0.2 convert_reduce_fusion
  19.5 0.1 select_reduce_fusion
  19.6 0.1 pad_add_fusion.1.order_ref
  19.6 0.0 copy-done.3
  19.6 0.0 copy-done.4
  19.7 0.1 pad_add_fusion.planes_ref
  19.7 0.1 maximum_maximum_fusion
  19.8 45.5 %all-to-all-done.arr_ref = bf16[128,3,3,4,384]{4,3,2,1,0:T(4,128)(2,1)S(1)} async-done(((bf16[128,3,3,4,384]{4,3,2,1,0:T(4,128)(2,1)}), bf16[128,3,3,4,384]{4,3,2,1,0:T(4,128)(2,1)S(1)}, u32[]{:S(2)}, u32[]{:S(2)}) %all-to-all-start) | async-done | bytes 3538976 | tf_op jit(solution)/shard_map/all_to_all | solution.py:432
  65.3 0.1 broadcast_in_dim.47.coef_ref
  65.4 12.8 %send_products.1 = (f32[48,5,8,384]{3,2,1,0:T(8,128)S(1)}, f32[8,96,8,384]{3,2,1,0:T(8,128)S(1)}) custom-call(s32[15]{0:T(128)S(1)} %pad_add_fusion.planes_ref, bf16[128,3,3,4,384]{4,3,2,1,0:T(4,128)(2,1)S(1)} %all-to-all-done.arr_ref, bf16[4,4,768,256]{3,2,1,0:T(8,128)(2,1)} %constant.74.wx_hbm), custom_call_target="tpu_custom_call" | custom-call | tf_op jit(solution)/shard_map/send_products/pallas_call | solution.py:280
  78.2 0.1 collective-permute-start
  78.3 0.0 copy-start
  78.3 4.5 %keep_products.1.keep_ref = f32[48,5,8,384]{3,2,1,0:T(8,128)S(1)} custom-call(s32[15]{0:T(128)S(1)} %pad_add_fusion.planes_ref, f32[8,96,8,384]{3,2,1,0:T(8,128)S(1)} %get-tuple-element.14.u_ref), custom_call_target="tpu_custom_call" | custom-call | flops 60000000 | bytes 12000000 | tf_op jit(solution)/shard_map/keep_products/pallas_call | solution.py:302
  82.8 0.8 collective-permute-done.other_ref
  83.6 0.0 copy-done
  83.6 6.8 %x_lags.1 = bf16[128,3,2,1408]{3,2,1,0:T(2,128)(2,1)S(1)} custom-call(s32[97]{0:T(128)S(1)} %pad_add_fusion.1.order_ref, f32[48,5,8,384]{3,2,1,0:T(8,128)S(1)} %keep_products.1.keep_ref, f32[48,5,8,384]{3,2,1,0:T(8,128)S(1)} %collective-permute-done.other_ref, bf16[768,512]{1,0:T(8,128)(2,1)S(1)} %copy-done, f32[3,8,384]{2,1,0:T(8,128)S(1)} %broadcast_in_dim.47.coef_ref), custom_call_target="tpu_custom_call" | custom-call | tf_op jit(solution)/shard_map/x_lags/pallas_call | solution.py:365
  90.4 0.0 copy-start.1
  90.5 33.4 %all_to_all.10.x_ref = bf16[128,3,2,1408]{3,2,1,0:T(2,128)(2,1)S(1)} all-to-all(bf16[128,3,2,1408]{3,2,1,0:T(2,128)(2,1)S(1)} %x_lags.1), channel_id=1, replica_groups=mesh['y'=4,'x'=4,'core'=2,'z'=4] {'core','y','x','z'}, dimensions={0} | all-to-all | bytes 4325376 | tf_op jit(solution)/shard_map/all_to_all | solution.py:459
  123.8 0.0 copy-done.1
  123.8 4.2 %z_lags.1 = f32[3,9,96,384]{3,2,1,0:T(8,128)} custom-call(bf16[128,3,2,1408]{3,2,1,0:T(2,128)(2,1)S(1)} %all_to_all.10.x_ref, bf16[384,384]{1,0:T(8,128)(2,1)S(1)} %copy-done.1), custom_call_target="tpu_custom_call" | custom-call | tf_op jit(solution)/shard_map/z_lags/pallas_call | solution.py:411
  (3 shorter events, 0.0 us)
Async XLA Ops:
  7.7 11.6 %copy-start.2 = (s32[48]{0:T(128)S(1)}, s32[48]{0:T(128)}, u32[]{:S(2)}) copy-start(s32[48]{0:T(128)} %param.11) | copy-start | bytes 580
  7.7 12.0 %copy-start.3 = (s32[8]{0:T(128)S(1)}, s32[8]{0:T(128)}, u32[]{:S(2)}) copy-start(s32[8]{0:T(128)} %param.10) | copy-start | bytes 100
  7.7 12.0 %copy-start.4 = (s32[6]{0:T(128)S(1)}, s32[6]{0:T(128)}, u32[]{:S(2)}) copy-start(s32[6]{0:T(128)} %param.9) | copy-start | bytes 76
  7.7 57.7 %all-to-all-start = ((bf16[128,3,3,4,384]{4,3,2,1,0:T(4,128)(2,1)}), bf16[128,3,3,4,384]{4,3,2,1,0:T(4,128)(2,1)S(1)}, u32[]{:S(2)}, u32[]{:S(2)}) async-start(bf16[128,3,3,4,384]{4,3,2,1,0:T(4,128)(2,1)} %z_transform.1), calls=%async_computation | async-start | bytes 7077888 | tf_op jit(solution)/shard_map/all_to_all | solution.py:432
  78.2 5.5 %collective-permute-start = (f32[48,5,8,384]{3,2,1,0:T(8,128)S(1)}, f32[48,5,8,384]{3,2,1,0:T(8,128)S(1)}, u32[]{:S(2)}, u32[]{:S(2)}) collective-permute-start(f32[48,5,8,384]{3,2,1,0:T(8,128)S(1)} %get-tuple-element.15), channel_id=1, source_target_pairs={{0,4},{4,0},{1,5},{5,1},{2,6},{6,2},{3,7},{7,3},{8,12},{12,8},{9,1... | collective-permute-start | bytes 8847368 | tf_op jit(solution)/shard_map/ppermute | solution.py:456
  78.3 5.4 %copy-start = (bf16[768,512]{1,0:T(8,128)(2,1)S(1)}, bf16[768,512]{1,0:T(8,128)(2,1)}, u32[]{:S(2)}) copy-start(bf16[768,512]{1,0:T(8,128)(2,1)} %constant.75.tx_ref) | copy-start | bytes 2359300
  90.4 33.4 %copy-start.1 = (bf16[384,384]{1,0:T(8,128)(2,1)S(1)}, bf16[384,384]{1,0:T(8,128)(2,1)}, u32[]{:S(2)}) copy-start(bf16[384,384]{1,0:T(8,128)(2,1)} %constant.76.table_ref) | copy-start | bytes 884740

commit v4 on v3

--- a/solution.py
+++ b/solution.py
@@ -194,10 +194,10 @@
                 left, right = {}, {}
                 for i in sorted({ij // 3 for ij in chosen}):
                     re, im = u_ref[m, first + i, :, at], u_ref[4 + m, first + i, :, at]
-                    left[i] = (re, im, re - im)
+                    left[i] = (re, im, u_ref[8 + m, first + i, :, at])
                 for j in range(3):
                     re, im = u_ref[m, second + j, :, at], u_ref[4 + m, second + j, :, at]
-                    right[j] = (re, im, re + im)
+                    right[j] = (re, im, u_ref[12 + m, second + j, :, at])
                 for ij in chosen:
                     terms = [a * b for a, b in zip(left[ij // 3], right[ij % 3])]
                     sums[ij] = terms if m == 0 else [s + t for s, t in zip(sums[ij], terms)]
@@ -208,7 +208,7 @@
                 out_ref[p, n, :, at] = jnp.where(low, re, im) + pltpu.roll(jnp.where(low, im, re), 4, 0)
         return carry
 
-    lax.fori_loop(0, PAIRS, pair_products, 0)
+    lax.fori_loop(0, PAIRS, pair_products, 0, unroll=2)
 
 
 def keep_kernel(planes_ref, u_ref, keep_ref):
@@ -254,7 +254,7 @@
                     lhs_ref[r, pl.ds(row, 16), part * LAG : (part + 1) * LAG] = both
         return carry
 
-    lax.fori_loop(0, NY // 2, butterfly, 0)
+    lax.fori_loop(0, NY // 2, butterfly, 0, unroll=2)
 
     lane = lax.broadcasted_iota(jnp.int32, (8, 128), 1)
 
@@ -270,7 +270,13 @@
                 for row in range(24 * r, 24 * r + 24):
                     for h in range(2):
                         v = side_by_side([done[q, row, :, h * 128 : (h + 1) * 128] for q in range(4)], lane)
-                        u_ref[2 * tile - 2 + h, row] = jnp.concatenate(v, axis=1)
+                        v = jnp.concatenate(v, axis=1)
+                        which = 2 * tile - 2 + h
+                        u_ref[which, row] = v
+                        if which >= 4:
+                            re = u_ref[which - 4, row]
+                            u_ref[which + 4, row] = re - v
+                            u_ref[which + 8, row] = re + v
 
     pair_loop(planes_ref, u_ref, send_ref, False)
 
@@ -283,7 +289,7 @@
         out_specs=[vmem, vmem],
         out_shape=[
             jax.ShapeDtypeStruct((PAIRS, 5, 8, LAG), F32),
-            jax.ShapeDtypeStruct((8, 3 * NY, 8, LAG), F32),
+            jax.ShapeDtypeStruct((16, 3 * NY, 8, LAG), F32),
         ],
         scratch_shapes=[
             pltpu.VMEM((4, 4, 2 * LAG, 256), BF16),
@@ -304,7 +310,7 @@
         in_specs=[pl.BlockSpec(memory_space=pltpu.SMEM), vmem],
         out_specs=vmem,
         out_shape=jax.ShapeDtypeStruct((PAIRS, 5, 8, LAG), F32),
-        cost_estimate=pl.CostEstimate(flops=60_000_000, bytes_accessed=12_000_000, transcendentals=0),
+        cost_estimate=pl.CostEstimate(flops=60_000_000, bytes_accessed=22_000_000, transcendentals=0),
         compiler_params=pltpu.CompilerParams(vmem_limit_bytes=8 * MIB),
         name="keep_products",
     )(planes, u)

time: 128 us -> 128 us (level)
  transfers between devices with their start and end apart: 2 -> 2, of which waited for: 2 -> 2; matrix products, arithmetic and copies ran while one was open for 0% -> 0% of each run, Pallas kernels for 4% -> 3%
where the time goes in v4:
time: 128 us
  waiting for transfers between devices  46.8 us (37%)
  Pallas kernels  35.2 us (28%)
  blocking collectives  33.4 us (26%)
  starting transfers between devices  11.6 us (9%)
    all_to_all x1, waiting for transfers between devices, per_device(): lax.all_to_all(parcels, ('y', 'x', 'core', 'z'), split_axis=0, concat_axi...  45.5 us
    all_to_all x1, blocking collectives, per_device(): lax.all_to_all(spread, ('core', 'y', 'x', 'z'), split_axis=0, concat_axis...  33.4 us
    pallas_call x1, Pallas kernels, send_products(): pl.pallas_call(send_kernel, in_specs=[pl.BlockSpec(memory_space=pltpu.SME...  12.4 us
    all_to_all x1, starting transfers between devices, per_device(): lax.all_to_all(parcels, ('y', 'x', 'core', 'z'), split_axis=0, concat_axi...  11.5 us
    pallas_call x1, Pallas kernels, z_transform(): pl.pallas_call(z_kernel, grid=(4,), in_specs=[pl.BlockSpec((NZ // 4, NZ /...  7.65 us
    pallas_call x1, Pallas kernels, x_lags(): pl.pallas_call(x_lag_kernel, in_specs=[pl.BlockSpec(memory_space=pltpu.SM...  6.82 us
    pallas_call x1, Pallas kernels, z_lags(): pl.pallas_call(z_lag_kernel, in_specs=[vmem, vmem], out_specs=pl.BlockSpe...  4.22 us
    pallas_call x1, Pallas kernels, keep_products(): pl.pallas_call(keep_kernel, in_specs=[pl.BlockSpec(memory_space=pltpu.SME...  4.02 us
  transfers between devices with their start and end apart: 2, of which 2 were waited for; matrix products, arithmetic and copies ran while one was open for 0% of the time, Pallas kernels for 3%

profile of v4, /device:TPU:1, one launch (start us, length us, event | category | flops | bytes accessed | tf_op | source)
XLA Modules:
  0.0 127.7 jit_solution(12555900513584392397)
XLA Ops:
  0.0 7.7 %z_transform.1 = bf16[128,3,3,4,384]{4,3,2,1,0:T(4,128)(2,1)} custom-call(bf16[1536,768]{1,0:T(8,128)(2,1)} %constant.73.table_ref, bf16[3,384,1536]{2,1,0:T(8,128)(2,1)} %bitcast.3), custom_call_target="tpu_custom_call" | custom-call | tf_op jit(solution)/shard_map/z_transform/pallas_call | solution.py:153
  7.7 0.0 copy-start.2
  7.7 0.0 copy-start.3
  7.7 0.0 copy-start.4
  7.7 11.5 %all-to-all-start = ((bf16[128,3,3,4,384]{4,3,2,1,0:T(4,128)(2,1)}), bf16[128,3,3,4,384]{4,3,2,1,0:T(4,128)(2,1)S(1)}, u32[]{:S(2)}, u32[]{:S(2)}) async-start(bf16[128,3,3,4,384]{4,3,2,1,0:T(4,128)(2,1)} %z_transform.1), calls=%async_computation | async-start | bytes 7077888 | tf_op jit(solution)/shard_map/all_to_all | solution.py:438
  19.2 0.1 pad.2.clone
  19.3 0.0 copy-done.2
  19.3 0.2 convert_reduce_fusion
  19.5 0.1 select_reduce_fusion
  19.6 0.1 pad_add_fusion.1.order_ref
  19.6 0.0 copy-done.3
  19.6 0.0 copy-done.4
  19.7 0.1 pad_add_fusion.planes_ref
  19.7 0.1 maximum_maximum_fusion
  19.8 45.5 %all-to-all-done.arr_ref = bf16[128,3,3,4,384]{4,3,2,1,0:T(4,128)(2,1)S(1)} async-done(((bf16[128,3,3,4,384]{4,3,2,1,0:T(4,128)(2,1)}), bf16[128,3,3,4,384]{4,3,2,1,0:T(4,128)(2,1)S(1)}, u32[]{:S(2)}, u32[]{:S(2)}) %all-to-all-start) | async-done | bytes 3538976 | tf_op jit(solution)/shard_map/all_to_all | solution.py:438
  65.3 0.1 broadcast_in_dim.47.coef_ref
  65.4 12.4 %send_products.1 = (f32[48,5,8,384]{3,2,1,0:T(8,128)S(1)}, f32[16,96,8,384]{3,2,1,0:T(8,128)S(1)}) custom-call(s32[15]{0:T(128)S(1)} %pad_add_fusion.planes_ref, bf16[128,3,3,4,384]{4,3,2,1,0:T(4,128)(2,1)S(1)} %all-to-all-done.arr_ref, bf16[4,4,768,256]{3,2,1,0:T(8,128)(2,1)} %constant.74.wx_hbm), custom_call_target="tpu_custom_call" | custom-call | tf_op jit(solution)/shard_map/send_products/pallas_call | solution.py:286
  77.8 0.1 collective-permute-start
  77.9 0.0 copy-start
  77.9 4.0 %keep_products.1.keep_ref = f32[48,5,8,384]{3,2,1,0:T(8,128)S(1)} custom-call(s32[15]{0:T(128)S(1)} %pad_add_fusion.planes_ref, f32[16,96,8,384]{3,2,1,0:T(8,128)S(1)} %get-tuple-element.14.u_ref), custom_call_target="tpu_custom_call" | custom-call | flops 60000000 | bytes 22000000 | tf_op jit(solution)/shard_map/keep_products/pallas_call | solution.py:308
  82.0 1.3 %collective-permute-done.other_ref = f32[48,5,8,384]{3,2,1,0:T(8,128)S(1)} collective-permute-done((f32[48,5,8,384]{3,2,1,0:T(8,128)S(1)}, f32[48,5,8,384]{3,2,1,0:T(8,128)S(1)}, u32[]{:S(2)}, u32[]{:S(2)}) %collective-permute-start) | collective-permute-done | bytes 2949152 | tf_op jit(solution)/shard_map/ppermute | solution.py:462
  83.3 0.0 copy-done
  83.3 6.8 %x_lags.1 = bf16[128,3,2,1408]{3,2,1,0:T(2,128)(2,1)S(1)} custom-call(s32[97]{0:T(128)S(1)} %pad_add_fusion.1.order_ref, f32[48,5,8,384]{3,2,1,0:T(8,128)S(1)} %keep_products.1.keep_ref, f32[48,5,8,384]{3,2,1,0:T(8,128)S(1)} %collective-permute-done.other_ref, bf16[768,512]{1,0:T(8,128)(2,1)S(1)} %copy-done, f32[3,8,384]{2,1,0:T(8,128)S(1)} %broadcast_in_dim.47.coef_ref), custom_call_target="tpu_custom_call" | custom-call | tf_op jit(solution)/shard_map/x_lags/pallas_call | solution.py:371
  90.1 0.0 copy-start.1
  90.1 33.4 %all_to_all.10.x_ref = bf16[128,3,2,1408]{3,2,1,0:T(2,128)(2,1)S(1)} all-to-all(bf16[128,3,2,1408]{3,2,1,0:T(2,128)(2,1)S(1)} %x_lags.1), channel_id=1, replica_groups=mesh['y'=4,'x'=4,'core'=2,'z'=4] {'core','y','x','z'}, dimensions={0} | all-to-all | bytes 4325376 | tf_op jit(solution)/shard_map/all_to_all | solution.py:465
  123.5 0.0 copy-done.1
  123.5 4.2 %z_lags.1 = f32[3,9,96,384]{3,2,1,0:T(8,128)} custom-call(bf16[128,3,2,1408]{3,2,1,0:T(2,128)(2,1)S(1)} %all_to_all.10.x_ref, bf16[384,384]{1,0:T(8,128)(2,1)S(1)} %copy-done.1), custom_call_target="tpu_custom_call" | custom-call | tf_op jit(solution)/shard_map/z_lags/pallas_call | solution.py:417
  (3 shorter events, 0.0 us)
Async XLA Ops:
  7.7 11.6 %copy-start.2 = (s32[48]{0:T(128)S(1)}, s32[48]{0:T(128)}, u32[]{:S(2)}) copy-start(s32[48]{0:T(128)} %param.11) | copy-start | bytes 580
  7.7 12.0 %copy-start.3 = (s32[8]{0:T(128)S(1)}, s32[8]{0:T(128)}, u32[]{:S(2)}) copy-start(s32[8]{0:T(128)} %param.10) | copy-start | bytes 100
  7.7 12.0 %copy-start.4 = (s32[6]{0:T(128)S(1)}, s32[6]{0:T(128)}, u32[]{:S(2)}) copy-start(s32[6]{0:T(128)} %param.9) | copy-start | bytes 76
  7.7 57.7 %all-to-all-start = ((bf16[128,3,3,4,384]{4,3,2,1,0:T(4,128)(2,1)}), bf16[128,3,3,4,384]{4,3,2,1,0:T(4,128)(2,1)S(1)}, u32[]{:S(2)}, u32[]{:S(2)}) async-start(bf16[128,3,3,4,384]{4,3,2,1,0:T(4,128)(2,1)} %z_transform.1), calls=%async_computation | async-start | bytes 7077888 | tf_op jit(solution)/shard_map/all_to_all | solution.py:438
  77.8 5.5 %collective-permute-start = (f32[48,5,8,384]{3,2,1,0:T(8,128)S(1)}, f32[48,5,8,384]{3,2,1,0:T(8,128)S(1)}, u32[]{:S(2)}, u32[]{:S(2)}) collective-permute-start(f32[48,5,8,384]{3,2,1,0:T(8,128)S(1)} %get-tuple-element.15), channel_id=1, source_target_pairs={{0,4},{4,0},{1,5},{5,1},{2,6},{6,2},{3,7},{7,3},{8,12},{12,8},{9,1... | collective-permute-start | bytes 8847368 | tf_op jit(solution)/shard_map/ppermute | solution.py:462
  77.9 5.4 %copy-start = (bf16[768,512]{1,0:T(8,128)(2,1)S(1)}, bf16[768,512]{1,0:T(8,128)(2,1)}, u32[]{:S(2)}) copy-start(bf16[768,512]{1,0:T(8,128)(2,1)} %constant.75.tx_ref) | copy-start | bytes 2359300
  90.1 33.4 %copy-start.1 = (bf16[384,384]{1,0:T(8,128)(2,1)S(1)}, bf16[384,384]{1,0:T(8,128)(2,1)}, u32[]{:S(2)}) copy-start(bf16[384,384]{1,0:T(8,128)(2,1)} %constant.76.table_ref) | copy-start | bytes 884740
